TPU v7x, 32 devices: a whole 2x2x4 slice. The times are simulated.
32 devices in a mesh: fsdp: 8 (over z, y), seq: 4 (over x, core).
Axes of the slice: x: 2, y: 2, z: 4, core: 2. Of those that a mesh axis runs over, the one named last changes fastest.
Arguments:
- tokens: bfloat16 [4096, 1152], P(('fsdp', 'seq')), may hold values from -6 to 6
- doc_start: int32 [4096], P(('fsdp', 'seq')), may hold values from 0 to 511, as said below
- gains: bfloat16 [5120], P(('fsdp', 'seq')), may hold values from 0.5 to 1.5
- w_query: bfloat16 [1152, 1024], P(None, ('fsdp', 'seq')), may hold values from -0.1875 to 0.1875
- w_key: bfloat16 [1152, 256], P(None, ('fsdp', 'seq')), may hold values from -0.1875 to 0.1875
- w_value: bfloat16 [1152, 256], P(None, ('fsdp', 'seq')), may hold values from -0.1875 to 0.1875
- w_out: bfloat16 [1024, 1152], P(('fsdp', 'seq')), may hold values from -0.1875 to 0.1875
- w_gate: bfloat16 [1152, 6912], P(None, ('fsdp', 'seq')), may hold values from -0.1875 to 0.1875
- w_up: bfloat16 [1152, 6912], P(None, ('fsdp', 'seq')), may hold values from -0.1875 to 0.1875
- w_down: bfloat16 [6912, 1152], P(('fsdp', 'seq')), may hold values from -0.078125 to 0.078125
- cotangent: bfloat16 [4096, 1152], P(('fsdp', 'seq')), may hold values from -6 to 6
Outputs:
- output: bfloat16 [4096, 1152], P(('fsdp', 'seq'))
- grad_tokens: float32 [4096, 1152], P(('fsdp', 'seq'))
- grad_gains: float32 [5120], P(('fsdp', 'seq'))
- grad_query: float32 [1152, 1024], P(None, ('fsdp', 'seq'))
- grad_key: float32 [1152, 256], P(None, ('fsdp', 'seq'))
- grad_value: float32 [1152, 256], P(None, ('fsdp', 'seq'))
- grad_out: float32 [1024, 1152], P(('fsdp', 'seq'))
- grad_gate: float32 [1152, 6912], P(None, ('fsdp', 'seq'))
- grad_up: float32 [1152, 6912], P(None, ('fsdp', 'seq'))
- grad_down: float32 [6912, 1152], P(('fsdp', 'seq'))
Inputs may be any that keep to these rules, and one draw needn't show every extreme that they name: For the token at place t of its sequence of 512 tokens, doc_start is the place where its document begins: t - 383 <= doc_start <= t, and it equals t or the previous token's value; the first token of a sequence begins a document, and every sequence holds one document of exactly 384 tokens.
All inputs are finite; a program needn't handle non-finite values.
Results may differ from a plain program's by a relative error of at most 0.019.
Values may be sent and summed in bfloat16 or wider, within the bound.
A program may use at most 256 MiB of HBM per device.

v0:
```python
from functools import partial

import jax
import jax.numpy as jnp
from jax import lax
from jax.sharding import PartitionSpec as P

norm_eps = 1e-06
rope_base = 1000000.0
score_scale = 0.0625
masked_value = -1e30


def product(former, latter):
    return jnp.dot(former, latter, preferred_element_type=jnp.float32)


def inner_rows(former, latter):
    return lax.dot_general(
        former, latter, (((0,), (0,)), ((), ())), preferred_element_type=jnp.float32
    )


def outer_rows(former, latter):
    return lax.dot_general(
        former, latter, (((1,), (1,)), ((), ())), preferred_element_type=jnp.float32
    )


def scaled_norm(values, factor):
    return values * lax.rsqrt(jnp.mean(values * values, axis=-1, keepdims=True) + norm_eps) * factor


def rotate(values, cos_table, sin_table):
    half_width = values.shape[-1] // 2
    leading = values[..., :half_width]
    trailing = values[..., half_width:]
    return jnp.concatenate(
        [leading * cos_table - trailing * sin_table, trailing * cos_table + leading * sin_table],
        axis=-1,
    )


def head_norm(values, factor, cos_table, sin_table):
    return rotate(scaled_norm(values, factor), cos_table, sin_table)


def gated_unit(gate_in, up_in):
    return jax.nn.gelu(gate_in, approximate=True) * up_in


def rope_tables(places, rot_width):
    half_width = rot_width // 2
    frequency = rope_base ** (-2.0 * jnp.arange(half_width, dtype=jnp.float32) / rot_width)
    angles = places.astype(jnp.float32)[:, None] * frequency[None, :]
    return (jnp.cos(angles)[:, None, :], jnp.sin(angles)[:, None, :])


def masked_scores(queries, key_rows, bounds, offset):
    raw_scores = outer_rows(queries, key_rows) * score_scale
    query_place = offset + jnp.arange(queries.shape[0], dtype=jnp.int32)
    key_place = jnp.arange(key_rows.shape[0], dtype=jnp.int32)
    allowed = (key_place[None, :] >= bounds[:, None]) & (key_place[None, :] <= query_place[:, None])
    return jnp.where(allowed, raw_scores, masked_value)


def local(
    tokens, doc_start, gains, w_query, w_key, w_value, w_out, w_gate, w_up, w_down, cotangent
):
    tok_rows = tokens.shape[0]
    model_width = tokens.shape[1]
    run_index = lax.axis_index("seq")
    gains_all, query_w, key_w, value_w, out_w = (
        lax.all_gather(gains, ("fsdp", "seq"), axis=0, tiled=True),
        lax.all_gather(w_query, ("fsdp", "seq"), axis=1, tiled=True),
        lax.all_gather(w_key, ("fsdp", "seq"), axis=1, tiled=True),
        lax.all_gather(w_value, ("fsdp", "seq"), axis=1, tiled=True),
        lax.all_gather(w_out, ("fsdp", "seq"), axis=0, tiled=True),
    )
    gate_w, up_w, down_w = (
        lax.all_gather(w_gate, ("fsdp", "seq"), axis=1, tiled=True),
        lax.all_gather(w_up, ("fsdp", "seq"), axis=1, tiled=True),
        lax.all_gather(w_down, ("fsdp", "seq"), axis=0, tiled=True),
    )
    head_width = key_w.shape[1]
    head_count = query_w.shape[1] // head_width
    gain_values = gains_all.astype(jnp.float32)
    gain_pre = gain_values[:model_width]
    gain_query = gain_values[model_width : model_width + head_width]
    gain_key = gain_values[model_width + head_width : model_width + 2 * head_width]
    gain_post = gain_values[model_width + 2 * head_width : 2 * model_width + 2 * head_width]
    gain_pre_ffn = gain_values[2 * model_width + 2 * head_width : 3 * model_width + 2 * head_width]
    gain_post_ffn = gain_values[3 * model_width + 2 * head_width :]
    residual = tokens.astype(jnp.float32)
    normed, pre_pull = jax.vjp(scaled_norm, residual, gain_pre)
    normed_b = normed.astype(jnp.bfloat16)
    query_raw = product(normed_b, query_w).reshape(tok_rows, head_count, head_width)
    key_raw = product(normed_b, key_w).reshape(tok_rows, 1, head_width)
    value_b = product(normed_b, value_w).astype(jnp.bfloat16)
    places = run_index * tok_rows + jnp.arange(tok_rows, dtype=jnp.int32) - doc_start
    cos_table, sin_table = rope_tables(places, head_width)
    rope_norm = partial(head_norm, cos_table=cos_table, sin_table=sin_table)
    query_rot, query_pull = jax.vjp(rope_norm, query_raw, gain_query)
    key_rot, key_pull = jax.vjp(rope_norm, key_raw, gain_key)
    query_b = query_rot.reshape(tok_rows, head_count * head_width).astype(jnp.bfloat16)
    key_b = key_rot.reshape(tok_rows, head_width).astype(jnp.bfloat16)
    query_heads = lax.all_to_all(query_b, "seq", split_axis=1, concat_axis=0, tiled=True)
    key_rows, value_rows = (
        lax.all_gather(key_b, "seq", axis=0, tiled=True),
        lax.all_gather(value_b, "seq", axis=0, tiled=True),
    )
    starts = lax.all_gather(doc_start, "seq", axis=0, tiled=True)
    seq_tokens = key_rows.shape[0]
    block_rows = min(512, seq_tokens)
    block_count = seq_tokens // block_rows
    query_blocks = query_heads.reshape(block_count, block_rows, head_width)
    start_blocks = starts.reshape(block_count, block_rows)
    block_ids = jnp.arange(block_count, dtype=jnp.int32)

    def attend(block_item):
        queries, bounds, block_index = block_item
        scores = masked_scores(queries, key_rows, bounds, block_index * block_rows)
        row_max = jnp.max(scores, axis=1, keepdims=True)
        weights = jnp.exp(scores - row_max)
        row_total = jnp.sum(weights, axis=1, keepdims=True)
        probability = (weights / row_total).astype(jnp.bfloat16)
        mixed_block = product(probability, value_rows).astype(jnp.bfloat16)
        return (mixed_block, (row_max + jnp.log(row_total))[:, 0])

    mixed_blocks, lse_blocks = lax.map(attend, (query_blocks, start_blocks, block_ids))
    mixed_heads = mixed_blocks.reshape(seq_tokens, head_width)
    mixed_tokens = lax.all_to_all(mixed_heads, "seq", split_axis=0, concat_axis=1, tiled=True)
    attn_raw = product(mixed_tokens, out_w)
    attn_out, post_pull = jax.vjp(scaled_norm, attn_raw, gain_post)
    middle = residual + attn_out
    normed_ffn, pre_ffn_pull = jax.vjp(scaled_norm, middle, gain_pre_ffn)
    normed_ffn_b = normed_ffn.astype(jnp.bfloat16)
    gate_act = product(normed_ffn_b, gate_w)
    up_act = product(normed_ffn_b, up_w)
    hidden, glu_pull = jax.vjp(gated_unit, gate_act, up_act)
    hidden_b = hidden.astype(jnp.bfloat16)
    ffn_raw = product(hidden_b, down_w)
    ffn_out, post_ffn_pull = jax.vjp(scaled_norm, ffn_raw, gain_post_ffn)
    result = (middle + ffn_out).astype(jnp.bfloat16)
    gate_w, up_w, down_w = (
        lax.all_gather(w_gate, ("fsdp", "seq"), axis=1, tiled=True),
        lax.all_gather(w_up, ("fsdp", "seq"), axis=1, tiled=True),
        lax.all_gather(w_down, ("fsdp", "seq"), axis=0, tiled=True),
    )
    query_w, key_w, value_w, out_w = (
        lax.all_gather(w_query, ("fsdp", "seq"), axis=1, tiled=True),
        lax.all_gather(w_key, ("fsdp", "seq"), axis=1, tiled=True),
        lax.all_gather(w_value, ("fsdp", "seq"), axis=1, tiled=True),
        lax.all_gather(w_out, ("fsdp", "seq"), axis=0, tiled=True),
    )
    upstream = cotangent.astype(jnp.float32)
    ffn_grad, gain_post_ffn_grad = post_ffn_pull(upstream)
    ffn_grad_b = ffn_grad.astype(jnp.bfloat16)
    down_w_grad = inner_rows(hidden_b, ffn_grad_b)
    hidden_grad = outer_rows(ffn_grad_b, down_w)
    gate_grad, up_grad = glu_pull(hidden_grad)
    gate_grad_b = gate_grad.astype(jnp.bfloat16)
    up_grad_b = up_grad.astype(jnp.bfloat16)
    gate_w_grad_t = inner_rows(gate_grad_b, normed_ffn_b)
    up_w_grad_t = inner_rows(up_grad_b, normed_ffn_b)
    normed_ffn_grad = outer_rows(gate_grad_b, gate_w) + outer_rows(up_grad_b, up_w)
    middle_part, gain_pre_ffn_grad = pre_ffn_pull(normed_ffn_grad)
    middle_grad = upstream + middle_part
    attn_grad, gain_post_grad = post_pull(middle_grad)
    attn_grad_b = attn_grad.astype(jnp.bfloat16)
    out_w_grad = inner_rows(mixed_tokens, attn_grad_b)
    mixed_grad = outer_rows(attn_grad_b, out_w).astype(jnp.bfloat16)
    mixed_grad_heads = lax.all_to_all(mixed_grad, "seq", split_axis=1, concat_axis=0, tiled=True)
    grad_blocks = mixed_grad_heads.reshape(block_count, block_rows, head_width)

    def attend_back(carried, block_item):
        key_accum, value_accum = carried
        queries, bounds, block_index, lse_row, block_grad = block_item
        scores = masked_scores(queries, key_rows, bounds, block_index * block_rows)
        probability = jnp.exp(scores - lse_row[:, None])
        prob_grad = outer_rows(block_grad, value_rows)
        value_accum = value_accum + inner_rows(probability.astype(jnp.bfloat16), block_grad)
        row_delta = jnp.sum(probability * prob_grad, axis=1, keepdims=True)
        score_grad = (probability * (prob_grad - row_delta)).astype(jnp.bfloat16)
        query_grad = product(score_grad, key_rows) * score_scale
        key_accum = key_accum + inner_rows(score_grad, queries) * score_scale
        return ((key_accum, value_accum), query_grad)

    zero_rows = jnp.zeros((seq_tokens, head_width), jnp.float32)
    (key_part, value_part), query_grad_blocks = lax.scan(
        attend_back,
        (zero_rows, zero_rows),
        (query_blocks, start_blocks, block_ids, lse_blocks, grad_blocks),
    )
    key_sum, value_sum = (
        lax.psum_scatter(
            key_part.astype(jnp.bfloat16), "seq", scatter_dimension=0, tiled=True
        ).astype(jnp.float32),
        lax.psum_scatter(
            value_part.astype(jnp.bfloat16), "seq", scatter_dimension=0, tiled=True
        ).astype(jnp.float32),
    )
    query_grad_tokens = lax.all_to_all(
        query_grad_blocks.reshape(seq_tokens, head_width).astype(jnp.bfloat16),
        "seq",
        split_axis=0,
        concat_axis=1,
        tiled=True,
    ).astype(jnp.float32)
    query_raw_grad, gain_query_grad = query_pull(
        query_grad_tokens.reshape(tok_rows, head_count, head_width)
    )
    key_raw_grad, gain_key_grad = key_pull(key_sum.reshape(tok_rows, 1, head_width))
    query_raw_b = query_raw_grad.reshape(tok_rows, head_count * head_width).astype(jnp.bfloat16)
    key_raw_b = key_raw_grad.reshape(tok_rows, head_width).astype(jnp.bfloat16)
    value_raw_b = value_sum.astype(jnp.bfloat16)
    query_w_grad_t = inner_rows(query_raw_b, normed_b)
    key_w_grad_t = inner_rows(key_raw_b, normed_b)
    value_w_grad_t = inner_rows(value_raw_b, normed_b)
    normed_grad = (
        outer_rows(query_raw_b, query_w)
        + outer_rows(key_raw_b, key_w)
        + outer_rows(value_raw_b, value_w)
    )
    residual_part, gain_pre_grad = pre_pull(normed_grad)
    input_grad = middle_grad + residual_part
    gains_grad = jnp.concatenate(
        [
            gain_pre_grad,
            gain_query_grad,
            gain_key_grad,
            gain_post_grad,
            gain_pre_ffn_grad,
            gain_post_ffn_grad,
        ]
    )
    shares = (
        lax.psum_scatter(gains_grad, ("fsdp", "seq"), scatter_dimension=0, tiled=True),
        lax.psum_scatter(query_w_grad_t, ("fsdp", "seq"), scatter_dimension=0, tiled=True),
        lax.psum_scatter(key_w_grad_t, ("fsdp", "seq"), scatter_dimension=0, tiled=True),
        lax.psum_scatter(value_w_grad_t, ("fsdp", "seq"), scatter_dimension=0, tiled=True),
        lax.psum_scatter(out_w_grad, ("fsdp", "seq"), scatter_dimension=0, tiled=True),
        lax.psum_scatter(gate_w_grad_t, ("fsdp", "seq"), scatter_dimension=0, tiled=True),
        lax.psum_scatter(up_w_grad_t, ("fsdp", "seq"), scatter_dimension=0, tiled=True),
        lax.psum_scatter(down_w_grad, ("fsdp", "seq"), scatter_dimension=0, tiled=True),
    )
    return (
        result,
        input_grad,
        shares[0],
        shares[1].T,
        shares[2].T,
        shares[3].T,
        shares[4],
        shares[5].T,
        shares[6].T,
        shares[7],
    )


def solution(mesh):
    in_specs = (
        P(("fsdp", "seq"), None),
        P(("fsdp", "seq")),
        P(("fsdp", "seq")),
        P(None, ("fsdp", "seq")),
        P(None, ("fsdp", "seq")),
        P(None, ("fsdp", "seq")),
        P(("fsdp", "seq"), None),
        P(None, ("fsdp", "seq")),
        P(None, ("fsdp", "seq")),
        P(("fsdp", "seq"), None),
        P(("fsdp", "seq"), None),
    )
    out_specs = (
        P(("fsdp", "seq"), None),
        P(("fsdp", "seq"), None),
        P(("fsdp", "seq")),
        P(None, ("fsdp", "seq")),
        P(None, ("fsdp", "seq")),
        P(None, ("fsdp", "seq")),
        P(("fsdp", "seq"), None),
        P(None, ("fsdp", "seq")),
        P(None, ("fsdp", "seq")),
        P(("fsdp", "seq"), None),
    )
    return jax.shard_map(local, mesh=mesh, in_specs=in_specs, out_specs=out_specs, check_vma=False)
```

profile of v0, /device:TPU:0, one launch (start us, length us, event | category | flops | bytes accessed | tf_op | source)
XLA Modules:
  0.0 1899.5 jit_solution(8101849914213547981)
XLA Ops:
  17.6 41.2 %all-reduce.4 = bf16[5120]{0:T(1024)(128)(2,1)S(1)} all-reduce(bf16[5120]{0:T(1024)(128)(2,1)S(1)} %dynamic-update-slice), channel_id=1, replica_groups=mesh['fsdp'=8,'seq'=4] {'fsdp','seq'}, use_global_device_ids=true, to_apply=%add.4 | all-reduce | flops 5120 | bytes 20480
  61.2 42.3 %all_gather.43 = bf16[1152,256]{0,1:T(8,128)(2,1)S(1)} all-gather(bf16[1152,8]{0,1:T(8,128)(2,1)} %param.15), channel_id=1, replica_groups=mesh['fsdp'=8,'seq'=4] {'fsdp','seq'}, dimensions={1}, use_global_device_ids=true | all-gather | bytes 608256 | tf_op jit(solution)/shard_map/all_gather | solution.py:76
  106.5 38.8 %all_gather.45 = bf16[1152,256]{0,1:T(8,128)(2,1)S(1)} all-gather(bf16[1152,8]{0,1:T(8,128)(2,1)S(1)} %copy-done.44), channel_id=1, replica_groups=mesh['fsdp'=8,'seq'=4] {'fsdp','seq'}, dimensions={1}, use_global_device_ids=true | all-gather | bytes 608256 | tf_op jit(solution)/shard_map/all_gather | solution.py:77
  185.8 61.2 %all-gather.12.cloned.1.call-done = bf16[1152,6912]{0,1:T(8,128)(2,1)} async-done(((bf16[1152,216]{0,1:T(8,128)(2,1)}), bf16[1152,6912]{0,1:T(8,128)(2,1)}) %all-gather.12.cloned.1.call-update) | async-done | bytes 15925264 | tf_op jit(solution)/shard_map/all_gather | solution.py:81
  247.0 11.7 fusion.71
  258.7 100.3 %all-gather.14.cloned.1.call-done = bf16[1152,6912]{0,1:T(8,128)(2,1)} async-done(((bf16[1152,216]{0,1:T(8,128)(2,1)}), bf16[1152,6912]{0,1:T(8,128)(2,1)}) %all-gather.14.cloned.1.call-update) | async-done | bytes 15925264 | tf_op jit(solution)/shard_map/all_gather | solution.py:82
  359.0 12.6 multiply_convert_fusion.1
  371.6 99.4 %all-gather.16.cloned.1.call-done = bf16[6912,1152]{1,0:T(8,128)(2,1)} async-done(((bf16[216,1152]{1,0:T(8,128)(2,1)}), bf16[6912,1152]{1,0:T(8,128)(2,1)}) %all-gather.16.cloned.1.call-update) | async-done | bytes 15925264 | tf_op jit(solution)/shard_map/all_gather | solution.py:83
  481.1 9.5 multiply_convert_fusion
  490.7 9.3 fusion.72
  500.1 8.9 multiply_reduce_fusion.1
  528.1 16.3 reduce-scatter.14.cloned.1.call-done
  550.6 16.4 reduce-scatter.16.cloned.1.call-done
  574.6 10.9 all_to_all.58
  592.9 13.9 fusion.75
  606.9 13.7 fusion.76
  621.5 12.6 fusion.77
  647.1 39.9 %all-reduce.5 = f32[5120]{0:T(1024)S(1)} all-reduce(f32[5120]{0:T(1024)} %constant_dynamic-update-slice_fusion), channel_id=5, replica_groups=mesh['fsdp'=8,'seq'=4] {'fsdp','seq'}, use_global_device_ids=true, to_apply=%region_23.24.clone | all-reduce | flops 5120 | bytes 40960
  688.7 19.6 %all-reduce.14.cloned.1.call-done = (f32[256,1152]{1,0:T(8,128)}, f32[256,1152]{1,0:T(8,128)}) async-done(((f32[256,1152]{1,0:T(8,128)}, f32[256,1152]{1,0:T(8,128)}), (f32[256,1152]{1,0:T(8,128)}, f32[256,1152]{1,0:T(8,128)})) %all-reduce.14.cloned.1.call-update) | async-done | bytes 2359312
  709.7 111.4 %reduce-scatter.20.cloned.1.call-done = f32[32,1152]{1,0:T(8,128)} async-done(((f32[1024,1152]{1,0:T(8,128)}), f32[32,1152]{1,0:T(8,128)}) %reduce-scatter.20.cloned.1.call-update) | async-done | bytes 147472 | tf_op jit(solution)/shard_map/reduce_scatter | solution.py:242
  821.1 112.0 %reduce-scatter.18.cloned.1.call-done = f32[32,1152]{1,0:T(8,128)} async-done(((f32[1024,1152]{1,0:T(8,128)}), f32[32,1152]{1,0:T(8,128)}) %reduce-scatter.18.cloned.1.call-update) | async-done | bytes 147472 | tf_op jit(solution)/shard_map/reduce_scatter | solution.py:239
  933.1 319.8 %reduce-scatter.22.cloned.1.call-done = f32[216,1152]{1,0:T(8,128)} async-done(((f32[6912,1152]{1,0:T(8,128)}), f32[216,1152]{1,0:T(8,128)}) %reduce-scatter.22.cloned.1.call-update) | async-done | bytes 995344
  1252.9 319.2 %reduce-scatter.24.cloned.1.call-done = f32[216,1152]{1,0:T(8,128)} async-done(((f32[6912,1152]{1,0:T(8,128)}), f32[216,1152]{1,0:T(8,128)}) %reduce-scatter.24.cloned.1.call-update) | async-done | bytes 995344
  1572.1 320.4 %reduce-scatter.26.cloned.1.call-done = f32[216,1152]{1,0:T(8,128)} async-done(((f32[6912,1152]{1,0:T(8,128)}), f32[216,1152]{1,0:T(8,128)}) %reduce-scatter.26.cloned.1.call-update) | async-done | bytes 995344
  (257 shorter events, 123.0 us)
Async XLA Ops:
  7.2 139.0 %copy-start = (bf16[128,1152]{1,0:T(8,128)(2,1)S(1)}, bf16[128,1152]{1,0:T(8,128)(2,1)}, u32[]{:S(2)}) copy-start(bf16[128,1152]{1,0:T(8,128)(2,1)} %param.11) | copy-start | bytes 884740
  7.2 99.3 %copy-start.44 = (bf16[1152,8]{0,1:T(8,128)(2,1)S(1)}, bf16[1152,8]{0,1:T(8,128)(2,1)}, u32[]{:S(2)}) copy-start(bf16[1152,8]{0,1:T(8,128)(2,1)} %param.16) | copy-start | bytes 55300
  7.2 139.4 %all-gather.8.cloned.1.call-start = ((), (), s32[]{:S(2)}) async-start(), calls=%async_computation.11 | async-start | bytes 2433024 | tf_op jit(solution)/shard_map/all_gather | solution.py:75
  7.9 168.2 %all-gather.10.cloned.1.call-start = ((), (), s32[]{:S(2)}) async-start(), calls=%async_computation.12 | async-start | bytes 2433024 | tf_op jit(solution)/shard_map/all_gather | solution.py:78
  8.7 238.3 %all-gather.12.cloned.1.call-start = ((), (), s32[]{:S(2)}) async-start(), calls=%async_computation.13 | async-start | bytes 16422912 | tf_op jit(solution)/shard_map/all_gather | solution.py:81
  9.4 349.6 %all-gather.14.cloned.1.call-start = ((), (), s32[]{:S(2)}) async-start(), calls=%async_computation.14 | async-start | bytes 16422912 | tf_op jit(solution)/shard_map/all_gather | solution.py:82
  10.0 461.0 %all-gather.16.cloned.1.call-start = ((), (), s32[]{:S(2)}) async-start(), calls=%async_computation.15 | async-start | bytes 16422912 | tf_op jit(solution)/shard_map/all_gather | solution.py:83
  58.8 87.8 %copy-start.57 = (f32[128]{0:T(128)}, f32[128]{0:T(128)S(1)}, u32[]{:S(2)}) copy-start(f32[128]{0:T(128)S(1)} %multiply_power_fusion) | copy-start | bytes 1540
  59.9 86.7 %copy-start.47 = (f32[128]{0:T(128)}, f32[128]{0:T(128)S(1)}, u32[]{:S(2)}) copy-start(f32[128]{0:T(128)S(1)} %fusion.52) | copy-start | bytes 1540
  60.6 86.0 %copy-start.58 = (f32[128]{0:T(128)}, f32[128]{0:T(128)S(1)}, u32[]{:S(2)}) copy-start(f32[128]{0:T(128)S(1)} %subtract_convert_fusion.1) | copy-start | bytes 1540
  61.2 124.2 %copy-start.36 = (f32[1152]{0:T(1024)}, f32[1152]{0:T(1024)S(1)}, u32[]{:S(2)}) copy-start(f32[1152]{0:T(1024)S(1)} %get-tuple-element.91) | copy-start | bytes 13828
  151.2 19.5 %all-to-all-start = ((bf16[128,4,256]{2,0,1:T(8,128)(2,1)}), bf16[128,4,256]{2,0,1:T(8,128)(2,1)S(1)}, u32[]{:S(2)}, u32[]{:S(2)}) async-start(bf16[128,4,256]{2,0,1:T(8,128)(2,1)} %pad_maximum_fusion), calls=%async_computation | async-start | bytes 524288 | tf_op jit(solution)/shard_map/all_to_all | solution.py:107
  172.5 9.6 all-to-all-start.1
  182.1 76.6 %copy-start.22 = (bf16[4,128,256]{1,2,0:T(8,128)(2,1)}, bf16[4,128,256]{1,2,0:T(8,128)(2,1)S(1)}, u32[]{:S(2)}) copy-start(bf16[4,128,256]{1,2,0:T(8,128)(2,1)S(1)} %all-to-all-done.1) | copy-start | bytes 786436
  184.9 73.8 %copy-start.60 = (f32[128]{0:T(128)}, f32[128]{0:T(128)S(1)}, u32[]{:S(2)}) copy-start(f32[128]{0:T(128)S(1)} %fusion.55) | copy-start | bytes 1540
  512.3 10.2 all-to-all-start.2
  516.4 28.0 %reduce-scatter.14.cloned.1.call-start = ((), (), s32[]{:S(2)}) async-start(), calls=%async_computation.16 | async-start | bytes 327680 | tf_op jit(solution)/shard_map/reduce_scatter | solution.py:196
  526.0 41.0 %reduce-scatter.16.cloned.1.call-start = ((), (), s32[]{:S(2)}) async-start(), calls=%async_computation.17 | async-start | bytes 327680 | tf_op jit(solution)/shard_map/reduce_scatter | solution.py:199
  528.0 180.3 %all-reduce.14.cloned.1.call-start = ((), (), s32[]{:S(2)}) async-start(), calls=%async_computation.23 | async-start | bytes 4718592
  569.3 251.8 %reduce-scatter.20.cloned.1.call-start = ((), (), s32[]{:S(2)}) async-start(), calls=%async_computation.19 | async-start | bytes 4866048 | tf_op jit(solution)/shard_map/reduce_scatter | solution.py:242
  572.4 360.7 %reduce-scatter.18.cloned.1.call-start = ((), (), s32[]{:S(2)}) async-start(), calls=%async_computation.18 | async-start | bytes 4866048 | tf_op jit(solution)/shard_map/reduce_scatter | solution.py:239
  592.9 660.0 %reduce-scatter.22.cloned.1.call-start = ((), (), s32[]{:S(2)}) async-start(), calls=%async_computation.20 | async-start | bytes 32845824
  606.8 965.2 %reduce-scatter.24.cloned.1.call-start = ((), (), s32[]{:S(2)}) async-start(), calls=%async_computation.21 | async-start | bytes 32845824
  620.6 1271.9 %reduce-scatter.26.cloned.1.call-start = ((), (), s32[]{:S(2)}) async-start(), calls=%async_computation.22 | async-start | bytes 32845824
  (63 other events, 843.0 us)
Sparse Core Ops, SparseCore 0:
  10.9 60.0 all-gather.7
  73.9 57.3 all-gather.9
  134.3 112.7 all-gather.11
  249.8 109.1 all-gather.13
  361.8 109.1 all-gather.15
  526.1 18.2 reduce-scatter.13
  547.0 20.0 reduce-scatter.15
  572.7 135.5 all-reduce.13
  715.3 105.8 reduce-scatter.19
  827.0 106.0 reduce-scatter.17
  941.2 311.6 reduce-scatter.21
  1259.8 312.2 reduce-scatter.23
  1580.2 312.2 reduce-scatter.25
where the time goes:
time: 1910 us; the launch traced here: 1900 us
  waiting for transfers between devices  1510 us (79%)
  blocking collectives  195 us (10%)
  matrix products  128 us (7%)
  local copies, waits for them, and re-layouts  22.2 us (1%)
    unnamed x17, waiting for transfers between devices  982 us
    reduce_scatter x1, waiting for transfers between devices, local(): lax.psum_scatter(query_w_grad_t, ('fsdp', 'seq'), scatter_dimension=0, ti...  112 us
    reduce_scatter x1, waiting for transfers between devices, local(): lax.psum_scatter(out_w_grad, ('fsdp', 'seq'), scatter_dimension=0, tiled=...  111 us
    all_gather x1, waiting for transfers between devices, local(): lax.all_gather(w_up, ('fsdp', 'seq'), axis=1, tiled=True)  100 us
    all_gather x1, waiting for transfers between devices, local(): lax.all_gather(w_down, ('fsdp', 'seq'), axis=0, tiled=True)  99.4 us
    unnamed x2, blocking collectives  81.1 us
    all_gather x1, waiting for transfers between devices, local(): lax.all_gather(w_gate, ('fsdp', 'seq'), axis=1, tiled=True)  61.2 us
    dot_general x9, matrix products, inner_rows(): lax.dot_general(former, latter, (((0,), (0,)), ((), ())), preferred_eleme...  53.4 us
  transfers between devices with their start and end apart: 16, of which 13 were waited for; matrix products, arithmetic and copies ran while one was open for 6% of the time, Pallas kernels for 0%

commit v1 on v0

--- a/solution.py
+++ b/solution.py
@@ -258,6 +258,172 @@
     )
 
 
+def gather_rows(block):
+    return lax.all_gather(block, ("fsdp", "seq"), axis=0, tiled=True)
+
+
+def scatter_rows(partial_sum):
+    return lax.psum_scatter(
+        partial_sum.astype(jnp.bfloat16), ("fsdp", "seq"), scatter_dimension=0, tiled=True
+    ).astype(jnp.float32)
+
+
+def split_model(
+    tokens, doc_start, gains, w_query, w_key, w_value, w_out, w_gate, w_up, w_down, cotangent
+):
+    tok_rows, model_width = tokens.shape
+    run_index = lax.axis_index("seq")
+    seq_count = lax.axis_size("seq")
+    dev_count = seq_count * lax.axis_size("fsdp")
+    query_rows, key_rows_own = w_query.shape[1], w_key.shape[1]
+    gain_row = jnp.pad(gains[None, :], ((0, 7), (0, model_width - gains.shape[0])))
+    packed = jnp.concatenate([w_query.T, w_out, w_key.T, w_value.T, gain_row], axis=0)
+    cuts = (query_rows, 2 * query_rows, 2 * query_rows + key_rows_own)
+    cuts = cuts + (cuts[2] + key_rows_own,)
+    everything = gather_rows(packed).reshape(dev_count, packed.shape[0], model_width)
+    query_t = everything[:, : cuts[0]].reshape(-1, model_width)
+    out_w = everything[:, cuts[0] : cuts[1]].reshape(-1, model_width)
+    key_t = everything[:, cuts[1] : cuts[2]].reshape(-1, model_width)
+    value_t = everything[:, cuts[2] : cuts[3]].reshape(-1, model_width)
+    gain_values = everything[:, cuts[3], : gains.shape[0]].reshape(-1).astype(jnp.float32)
+    head_width = key_t.shape[0]
+    head_count = query_t.shape[0] // head_width
+    places_in = [0, model_width, model_width + head_width, model_width + 2 * head_width]
+    places_in += [places_in[3] + model_width, places_in[3] + 2 * model_width, gain_values.shape[0]]
+    places_in[5:] = [places_in[4] + model_width, places_in[4] + 2 * model_width]
+    gain_pre, gain_query, gain_key, gain_post, gain_pre_ffn, gain_post_ffn = (
+        gain_values[first:last] for first, last in zip(places_in[:-1], places_in[1:])
+    )
+    residual = tokens.astype(jnp.float32)
+    normed, pre_pull = jax.vjp(scaled_norm, residual, gain_pre)
+    normed_b = normed.astype(jnp.bfloat16)
+    query_raw = outer_rows(normed_b, query_t).reshape(tok_rows, head_count, head_width)
+    key_raw = outer_rows(normed_b, key_t).reshape(tok_rows, 1, head_width)
+    value_b = outer_rows(normed_b, value_t).astype(jnp.bfloat16)
+    places = run_index * tok_rows + jnp.arange(tok_rows, dtype=jnp.int32) - doc_start
+    cos_table, sin_table = rope_tables(places, head_width)
+    rope_norm = partial(head_norm, cos_table=cos_table, sin_table=sin_table)
+    query_rot, query_pull = jax.vjp(rope_norm, query_raw, gain_query)
+    key_rot, key_pull = jax.vjp(rope_norm, key_raw, gain_key)
+    query_b = query_rot.astype(jnp.bfloat16).transpose(1, 0, 2).reshape(-1, head_width)
+    key_b = key_rot.reshape(tok_rows, head_width).astype(jnp.bfloat16)
+    both = lax.all_gather(jnp.concatenate([key_b, value_b], axis=1), "seq", axis=0, tiled=True)
+    key_rows, value_rows = both[:, :head_width], both[:, head_width:]
+    raw_scores = outer_rows(query_b, key_rows) * score_scale
+    query_place = run_index * tok_rows + jnp.arange(tok_rows, dtype=jnp.int32)
+    key_place = jnp.arange(key_rows.shape[0], dtype=jnp.int32)
+    allowed = (key_place[None, :] >= doc_start[:, None]) & (
+        key_place[None, :] <= query_place[:, None]
+    )
+    allowed = jnp.tile(allowed, (head_count, 1))
+    scores = jnp.where(allowed, raw_scores, masked_value)
+    row_max = jnp.max(scores, axis=1, keepdims=True)
+    weights = jnp.exp(scores - row_max)
+    probability = weights / jnp.sum(weights, axis=1, keepdims=True)
+    probability_b = probability.astype(jnp.bfloat16)
+    mixed = product(probability_b, value_rows).astype(jnp.bfloat16)
+    mixed_tokens = (
+        mixed.reshape(head_count, tok_rows, head_width).transpose(1, 0, 2).reshape(tok_rows, -1)
+    )
+    attn_raw = product(mixed_tokens, out_w)
+    attn_out, post_pull = jax.vjp(scaled_norm, attn_raw, gain_post)
+    middle = residual + attn_out
+    normed_ffn, pre_ffn_pull = jax.vjp(scaled_norm, middle, gain_pre_ffn)
+    normed_all = gather_rows(normed_ffn.astype(jnp.bfloat16))
+    gate_act = outer_rows(normed_all, w_gate.T)
+    up_act = outer_rows(normed_all, w_up.T)
+    hidden, glu_pull = jax.vjp(gated_unit, gate_act, up_act)
+    hidden_b = hidden.astype(jnp.bfloat16)
+    ffn_raw = scatter_rows(product(hidden_b, w_down))
+    ffn_out, post_ffn_pull = jax.vjp(scaled_norm, ffn_raw, gain_post_ffn)
+    result = (middle + ffn_out).astype(jnp.bfloat16)
+    upstream = cotangent.astype(jnp.float32)
+    ffn_grad, gain_post_ffn_grad = post_ffn_pull(upstream)
+    ffn_grad_all = gather_rows(ffn_grad.astype(jnp.bfloat16))
+    down_grad = inner_rows(hidden_b, ffn_grad_all)
+    hidden_grad = outer_rows(ffn_grad_all, w_down)
+    gate_grad, up_grad = glu_pull(hidden_grad)
+    gate_grad_b = gate_grad.astype(jnp.bfloat16)
+    up_grad_b = up_grad.astype(jnp.bfloat16)
+    gate_w_grad_t = inner_rows(gate_grad_b, normed_all)
+    up_w_grad_t = inner_rows(up_grad_b, normed_all)
+    normed_ffn_grad = scatter_rows(product(gate_grad_b, w_gate.T) + product(up_grad_b, w_up.T))
+    middle_part, gain_pre_ffn_grad = pre_ffn_pull(normed_ffn_grad)
+    middle_grad = upstream + middle_part
+    attn_grad, gain_post_grad = post_pull(middle_grad)
+    attn_grad_b = attn_grad.astype(jnp.bfloat16)
+    out_w_grad = inner_rows(mixed_tokens, attn_grad_b)
+    mixed_grad = outer_rows(attn_grad_b, out_w).astype(jnp.bfloat16)
+    mixed_grad = (
+        mixed_grad.reshape(tok_rows, head_count, head_width)
+        .transpose(1, 0, 2)
+        .reshape(-1, head_width)
+    )
+    prob_grad = outer_rows(mixed_grad, value_rows)
+    value_part = inner_rows(probability_b, mixed_grad)
+    row_delta = jnp.sum(probability * prob_grad, axis=1, keepdims=True)
+    score_grad = (probability * (prob_grad - row_delta)).astype(jnp.bfloat16)
+    query_grad = product(score_grad, key_rows) * score_scale
+    key_part = inner_rows(score_grad, query_b) * score_scale
+    both_sum = lax.psum_scatter(
+        jnp.concatenate([key_part, value_part], axis=1).astype(jnp.bfloat16),
+        "seq",
+        scatter_dimension=0,
+        tiled=True,
+    ).astype(jnp.float32)
+    query_raw_grad, gain_query_grad = query_pull(
+        query_grad.reshape(head_count, tok_rows, head_width).transpose(1, 0, 2)
+    )
+    key_raw_grad, gain_key_grad = key_pull(both_sum[:, None, :head_width])
+    query_raw_b = query_raw_grad.reshape(tok_rows, -1).astype(jnp.bfloat16)
+    key_raw_b = key_raw_grad.reshape(tok_rows, head_width).astype(jnp.bfloat16)
+    value_raw_b = both_sum[:, head_width:].astype(jnp.bfloat16)
+    normed_grad = (
+        product(query_raw_b, query_t) + product(key_raw_b, key_t) + product(value_raw_b, value_t)
+    )
+    residual_part, gain_pre_grad = pre_pull(normed_grad)
+    input_grad = middle_grad + residual_part
+    gains_grad = jnp.concatenate(
+        [
+            gain_pre_grad,
+            gain_query_grad,
+            gain_key_grad,
+            gain_post_grad,
+            gain_pre_ffn_grad,
+            gain_post_ffn_grad,
+        ]
+    )
+    gains_block = jnp.pad(
+        gains_grad.reshape(dev_count, 1, -1),
+        ((0, 0), (0, 7), (0, model_width - gains.shape[0])),
+    )
+    by_device = lambda rows: rows.reshape(dev_count, -1, model_width)
+    shares = scatter_rows(
+        jnp.concatenate(
+            [
+                by_device(inner_rows(query_raw_b, normed_b)),
+                by_device(out_w_grad),
+                by_device(inner_rows(key_raw_b, normed_b)),
+                by_device(inner_rows(value_raw_b, normed_b)),
+                gains_block,
+            ],
+            axis=1,
+        ).reshape(-1, model_width)
+    )
+    return (
+        result,
+        input_grad,
+        shares[cuts[3], : gains.shape[0]],
+        shares[: cuts[0]].T,
+        shares[cuts[1] : cuts[2]].T,
+        shares[cuts[2] : cuts[3]].T,
+        shares[cuts[0] : cuts[1]],
+        gate_w_grad_t.T,
+        up_w_grad_t.T,
+        down_grad,
+    )
+
+
 def solution(mesh):
     in_specs = (
         P(("fsdp", "seq"), None),
@@ -284,4 +450,5 @@
         P(None, ("fsdp", "seq")),
         P(("fsdp", "seq"), None),
     )
-    return jax.shard_map(local, mesh=mesh, in_specs=in_specs, out_specs=out_specs, check_vma=False)
+    body = split_model if mesh.size <= 32 else local
+    return jax.shard_map(body, mesh=mesh, in_specs=in_specs, out_specs=out_specs, check_vma=False)

time: 1910 us -> 763 us (0.40)
  waiting for transfers between devices: 1510 us -> 599 us
  blocking collectives: 195 us -> 7.21 us
  matrix products: 128 us -> 89.4 us
    unnamed x17 -> x8, waiting for transfers between devices: 982 us -> 89.2 us
    all_gather x5 -> x1, blocking collectives: 103 us -> 7.21 us  [split_model(): lax.all_gather(jnp.concatenate([key_b, value_b], axis=1), 'seq', axis=0,...]
    unnamed x2 -> x0, blocking collectives: 81.1 us -> none
    all_gather x5 -> x3, waiting for transfers between devices: 261 us -> 232 us  [gather_rows(): return lax.all_gather(block, ('fsdp', 'seq'), axis=0, tiled=True)]
    dot_general x9, matrix products: 53.4 us -> 27 us  [inner_rows(): lax.dot_general(former, latter, (((0,), (0,)), ((), ())), preferred_eleme...]
    reduce_scatter x4 -> x3, waiting for transfers between devices: 256 us -> 277 us  [the longest x2 268 us: scatter_rows(): lax.psum_scatter(partial_sum.astype(jnp.bfloat16), ('fsdp', 'seq'), scatt...]
  transfers between devices with their start and end apart: 16 -> 7, of which waited for: 13 -> 7; matrix products, arithmetic and copies ran while one was open for 6% -> 4% of each run, Pallas kernels for 0% -> 0%
where the time goes in v1:
time: 763 us; the launch traced here: 762 us
  waiting for transfers between devices  599 us (79%)
  matrix products  89.4 us (12%)
  other arithmetic  25.9 us (3%)
  local copies, waits for them, and re-layouts  24.5 us (3%)
  between operations  15.1 us (2%)
    reduce_scatter x2, waiting for transfers between devices, scatter_rows(): lax.psum_scatter(partial_sum.astype(jnp.bfloat16), ('fsdp', 'seq'), scatt...  268 us
    all_gather x3, waiting for transfers between devices, gather_rows(): return lax.all_gather(block, ('fsdp', 'seq'), axis=0, tiled=True)  232 us
    unnamed x8, waiting for transfers between devices  89.2 us
    dot_general x9, matrix products, product(): return jnp.dot(former, latter, preferred_element_type=jnp.float32)  32 us
    dot_general x9, matrix products, outer_rows(): lax.dot_general(former, latter, (((1,), (1,)), ((), ())), preferred_eleme...  30.4 us
    dot_general x9, matrix products, inner_rows(): lax.dot_general(former, latter, (((0,), (0,)), ((), ())), preferred_eleme...  27 us
  transfers between devices with their start and end apart: 7, of which 7 were waited for; matrix products, arithmetic and copies ran while one was open for 4% of the time, Pallas kernels for 0%

profile of v1, /device:TPU:0, one launch (start us, length us, event | category | flops | bytes accessed | tf_op | source)
XLA Modules:
  0.0 761.6 jit_solution(10266501291321799158)
XLA Ops:
  14.8 70.3 %all-gather.4.cloned.1.call-done = bf16[2816,1152]{1,0:T(8,128)(2,1)} async-done(((bf16[88,1152]{1,0:T(8,128)(2,1)}), bf16[2816,1152]{1,0:T(8,128)(2,1)}) %all-gather.4.cloned.1.call-update) | async-done | bytes 6488080 | tf_op jit(solution)/shard_map/all_gather | solution.py:262
  89.4 4.2 fusion.89
  94.6 7.2 all_gather.13
  107.6 2.4 multiply_reduce_fusion.4
  112.8 80.7 %all-gather.6.cloned.1.call-done = bf16[4096,1152]{1,0:T(8,128)(2,1)} async-done(((bf16[128,1152]{1,0:T(8,128)(2,1)}), bf16[4096,1152]{1,0:T(8,128)(2,1)}) %all-gather.6.cloned.1.call-update) | async-done | bytes 9437200 | tf_op jit(solution)/shard_map/all_gather | solution.py:262
  193.5 7.1 fusion.93
  200.7 5.2 multiply_convert_fusion.1
  207.1 5.4 convolution_convert_fusion
  212.8 134.0 %reduce-scatter.7.cloned.1.call-done = bf16[128,1152]{1,0:T(8,128)(2,1)} async-done(((bf16[4096,1152]{1,0:T(8,128)(2,1)}), bf16[128,1152]{1,0:T(8,128)(2,1)}) %reduce-scatter.7.cloned.1.call-update) | async-done | bytes 294928 | tf_op jit(solution)/shard_map/reduce_scatter | solution.py:266
  351.6 81.4 %all-gather.8.cloned.1.call-done = bf16[4096,1152]{1,0:T(8,128)(2,1)} async-done(((bf16[128,1152]{1,0:T(8,128)(2,1)}), bf16[4096,1152]{1,0:T(8,128)(2,1)}) %all-gather.8.cloned.1.call-update) | async-done | bytes 9437200 | tf_op jit(solution)/shard_map/all_gather | solution.py:262
  433.0 11.8 %multiply_convert_fusion = (bf16[4096,216]{0,1:T(8,128)(2,1)S(1)}, bf16[4096,216]{0,1:T(8,128)(2,1)S(1)}) fusion(f32[4096,216]{0,1:T(8,128)} %copy-done.68, f32[4096,216]{0,1:T(8,128)} %get-tuple-element.57, bf16[4096,1152]{1,0:T(8,128)(2,1)} %all-gather.8.cloned.1.call-done, bf16[216,1152]{1,0:T(8,128)(2,1)S(1)} %copy-done), kind=kOutput, calls=%fused_computation.16 | convolution fusion | flops 2059665408 | bytes 20551680 | tf_op jit(solution)/shard_map/dot_general | solution.py:25
  444.8 8.1 %fusion.94 = f32[4096,1152]{1,0:T(8,128)} fusion(bf16[4096,216]{0,1:T(8,128)(2,1)S(1)} %get-tuple-element.26, bf16[1152,216]{0,1:T(8,128)(2,1)S(1)} %copy-done.26), kind=kOutput, calls=%fused_computation.187 | convolution fusion | flops 2038431744 | bytes 21141504 | tf_op jit(solution)/shard_map/dot_general | solution.py:15
  452.9 10.3 %fusion = bf16[4096,1152]{1,0:T(8,128)(2,1)} fusion(f32[4096,1152]{1,0:T(8,128)} %fusion.94, bf16[4096,216]{0,1:T(8,128)(2,1)S(1)} %get-tuple-element.25, bf16[1152,216]{0,1:T(8,128)(2,1)S(1)} %copy-done.28), kind=kOutput, calls=%fused_computation.1 | convolution fusion | flops 2047868928 | bytes 30578688 | tf_op jit(solution)/shard_map/dot_general | solution.py:15
  463.4 134.2 %reduce-scatter.9.cloned.1.call-done = bf16[128,1152]{1,0:T(8,128)(2,1)} async-done(((bf16[4096,1152]{1,0:T(8,128)(2,1)}), bf16[128,1152]{1,0:T(8,128)(2,1)}) %reduce-scatter.9.cloned.1.call-update) | async-done | bytes 294928 | tf_op jit(solution)/shard_map/reduce_scatter | solution.py:266
  597.5 2.1 fusion.28
  599.7 3.2 multiply_reduce_fusion.1
  610.9 2.0 fusion.37
  614.1 2.2 fusion.2
  616.4 3.2 fusion.1
  621.0 9.3 %reduce-scatter.11.cloned.1.call-done = bf16[128,512]{1,0:T(8,128)(2,1)} async-done(((bf16[512,512]{1,0:T(8,128)(2,1)}), bf16[128,512]{1,0:T(8,128)(2,1)}) %reduce-scatter.11.cloned.1.call-update) | async-done | bytes 131088 | tf_op jit(solution)/shard_map/reduce_scatter | solution.py:368
  641.0 7.3 fusion.98
  648.3 7.6 %fusion.97 = f32[1152,216]{0,1:T(8,128)} fusion(bf16[4096,1152]{1,0:T(8,128)(2,1)} %all-gather.6.cloned.1.call-done, bf16[4096,216]{0,1:T(8,128)(2,1)S(1)} %copy-done.19), kind=kOutput, calls=%fused_computation.190 | convolution fusion | flops 2038431744 | bytes 12201984 | tf_op jit(solution)/shard_map/dot_general | solution.py:19
  656.0 3.5 fusion.96
  660.6 89.1 %reduce-scatter.13.cloned.1.call-done = bf16[88,1152]{1,0:T(8,128)(2,1)} async-done(((bf16[2816,1152]{1,0:T(8,128)(2,1)}), bf16[88,1152]{1,0:T(8,128)(2,1)}) %reduce-scatter.13.cloned.1.call-update) | async-done | bytes 202768
  (243 shorter events, 54.6 us)
Async XLA Ops:
  7.2 199.9 %copy-start = (bf16[216,1152]{1,0:T(8,128)(2,1)S(1)}, bf16[216,1152]{1,0:T(8,128)(2,1)}, u32[]{:S(2)}) copy-start(bf16[216,1152]{1,0:T(8,128)(2,1)} %param.20) | copy-start | bytes 1492996
  7.2 77.9 %all-gather.4.cloned.1.call-start = ((), (), s32[]{:S(2)}) async-start(), calls=%async_computation.4 | async-start | bytes 6690816 | tf_op jit(solution)/shard_map/all_gather | solution.py:262
  11.9 181.6 %all-gather.6.cloned.1.call-start = ((), (), s32[]{:S(2)}) async-start(), calls=%async_computation.5 | async-start | bytes 9732096 | tf_op jit(solution)/shard_map/all_gather | solution.py:262
  12.0 82.3 %copy-start.49 = (f32[128]{0:T(128)}, f32[128]{0:T(128)S(1)}, u32[]{:S(2)}) copy-start(f32[128]{0:T(128)S(1)} %multiply_power_fusion) | copy-start | bytes 1540
  13.1 80.5 %copy-start.61 = (f32[128]{0:T(128)}, f32[128]{0:T(128)S(1)}, u32[]{:S(2)}) copy-start(f32[128]{0:T(128)S(1)} %fusion.35) | copy-start | bytes 1540
  13.1 80.5 %copy-start.47 = (f32[128]{0:T(128)}, f32[128]{0:T(128)S(1)}, u32[]{:S(2)}) copy-start(f32[128]{0:T(128)S(1)} %fusion.76) | copy-start | bytes 1540
  14.8 88.8 %copy-start.22 = (f32[128,128]{1,0:T(8,128)}, f32[128,128]{1,0:T(8,128)S(1)}, u32[]{:S(2)}) copy-start(f32[128,128]{1,0:T(8,128)S(1)} %get-tuple-element.47) | copy-start | bytes 196612
  107.6 93.0 %copy-start.15 = (bf16[4,128,256]{1,2,0:T(8,128)(2,1)}, bf16[4,128,256]{1,2,0:T(8,128)(2,1)S(1)}, u32[]{:S(2)}) copy-start(bf16[4,128,256]{1,2,0:T(8,128)(2,1)S(1)} %copy.31) | copy-start | bytes 786436
  110.0 90.6 %copy-start.53 = (f32[128]{0:T(128)}, f32[128]{0:T(128)S(1)}, u32[]{:S(2)}) copy-start(f32[128]{0:T(128)S(1)} %fusion.78) | copy-start | bytes 1540
  111.1 89.5 %copy-start.59 = (f32[128]{0:T(128)}, f32[128]{0:T(128)S(1)}, u32[]{:S(2)}) copy-start(f32[128]{0:T(128)S(1)} %get-tuple-element.23) | copy-start | bytes 1540
  111.1 89.5 %copy-start.55 = (f32[128]{0:T(128)}, f32[128]{0:T(128)S(1)}, u32[]{:S(2)}) copy-start(f32[128]{0:T(128)S(1)} %fusion.79) | copy-start | bytes 1540
  112.8 234.0 %reduce-scatter.7.cloned.1.call-start = ((), (), s32[]{:S(2)}) async-start(), calls=%async_computation.6 | async-start | bytes 9732096 | tf_op jit(solution)/shard_map/reduce_scatter | solution.py:266
  212.5 135.3 %copy-start.14 = (bf16[128,1152]{1,0:T(8,128)(2,1)S(1)}, bf16[128,1152]{1,0:T(8,128)(2,1)}, u32[]{:S(2)}) copy-start(bf16[128,1152]{1,0:T(8,128)(2,1)} %param.21) | copy-start | bytes 884740
  212.5 220.4 %all-gather.8.cloned.1.call-start = ((), (), s32[]{:S(2)}) async-start(), calls=%async_computation.7 | async-start | bytes 9732096 | tf_op jit(solution)/shard_map/all_gather | solution.py:262
  351.6 246.0 %reduce-scatter.9.cloned.1.call-start = ((), (), s32[]{:S(2)}) async-start(), calls=%async_computation.8 | async-start | bytes 9732096 | tf_op jit(solution)/shard_map/reduce_scatter | solution.py:266
  463.3 134.3 %copy-start.56 = (f32[128]{0:T(128)S(1)}, f32[128]{0:T(128)}, u32[]{:S(2)}) copy-start(f32[128]{0:T(128)} %copy-done.55) | copy-start | bytes 1540
  463.3 136.4 %copy-start.60 = (f32[128]{0:T(128)S(1)}, f32[128]{0:T(128)}, u32[]{:S(2)}) copy-start(f32[128]{0:T(128)} %copy-done.59) | copy-start | bytes 1540
  463.3 136.4 %copy-start.9 = (bf16[128,1152]{1,0:T(8,128)(2,1)S(1)}, bf16[128,1152]{1,0:T(8,128)(2,1)}, u32[]{:S(2)}) copy-start(bf16[128,1152]{1,0:T(8,128)(2,1)} %reduce-scatter.7.cloned.1.call-done) | copy-start | bytes 884740
  463.3 136.4 %copy-start.54 = (f32[128]{0:T(128)S(1)}, f32[128]{0:T(128)}, u32[]{:S(2)}) copy-start(f32[128]{0:T(128)} %copy-done.53) | copy-start | bytes 1540
  463.3 136.4 %copy-start.58 = (f32[128]{0:T(128)S(1)}, f32[128]{0:T(128)}, u32[]{:S(2)}) copy-start(f32[128]{0:T(128)} %copy-done.57) | copy-start | bytes 1540
  463.3 139.6 %copy-start.64 = (f32[128]{0:T(128)S(1)}, f32[128]{0:T(128)}, u32[]{:S(2)}) copy-start(f32[128]{0:T(128)} %copy-done.63) | copy-start | bytes 1540
  463.3 167.0 %reduce-scatter.11.cloned.1.call-start = ((), (), s32[]{:S(2)}) async-start(), calls=%async_computation.9 | async-start | bytes 655360 | tf_op jit(solution)/shard_map/reduce_scatter | solution.py:368
  609.5 140.2 %reduce-scatter.13.cloned.1.call-start = ((), (), s32[]{:S(2)}) async-start(), calls=%async_computation.10 | async-start | bytes 6690816
  656.0 98.8 %copy-start.1 = (bf16[216,1152]{1,0:T(8,128)(2,1)S(1)}, bf16[216,1152]{1,0:T(8,128)(2,1)}, u32[]{:S(2)}) copy-start(bf16[216,1152]{1,0:T(8,128)(2,1)} %param.20) | copy-start | bytes 1492996
  (55 other events, 466.3 us)
Sparse Core Ops, SparseCore 0:
  12.0 73.0 all-gather.3
  112.9 80.5 all-gather.5
  212.7 134.0 reduce-scatter.6
  351.7 81.2 all-gather.7
  463.4 134.0 reduce-scatter.8
  609.6 20.6 reduce-scatter.10
  640.4 109.3 reduce-scatter.12

commit v2 on v1

--- a/solution.py
+++ b/solution.py
@@ -3,6 +3,8 @@
 import jax
 import jax.numpy as jnp
 from jax import lax
+from jax.experimental import pallas as pl
+from jax.experimental.pallas import tpu as pltpu
 from jax.sharding import PartitionSpec as P
 
 norm_eps = 1e-06
@@ -258,6 +260,410 @@
     )
 
 
+gelu_c = 0.7978845608028654
+MESH = pl.DeviceIdType.MESH
+DMA = pltpu.SemaphoreType.DMA
+
+
+def nt(former, latter):
+    return lax.dot_general(
+        former, latter, (((1,), (1,)), ((), ())), preferred_element_type=jnp.float32
+    )
+
+
+def nn(former, latter):
+    return lax.dot_general(
+        former, latter, (((1,), (0,)), ((), ())), preferred_element_type=jnp.float32
+    )
+
+
+def tn(former, latter):
+    return lax.dot_general(
+        former, latter, (((0,), (0,)), ((), ())), preferred_element_type=jnp.float32
+    )
+
+
+class Place:
+    def __init__(self):
+        self.f = lax.axis_index("fsdp")
+        self.s = lax.axis_index("seq")
+        self.z = self.f // 2
+        self.y = lax.rem(self.f, 2)
+        self.core = lax.rem(self.s, 2)
+        self.high = self.z // 2
+        self.inner = self.z * (3 - self.z) == 2
+        self.outer = self.z * (3 - self.z) == 0
+        self.sibling = (self.f, self.s + 1 - 2 * self.core)
+        self.over_x = (self.f, lax.rem(self.s + 2, 4))
+        self.over_y = (self.f + 1 - 2 * self.y, self.s)
+        self.toward = 1 - 2 * self.high
+
+    def at_z(self, z):
+        return (z * 2 + self.y, self.s)
+
+    def source(self, j):
+        last = j // 3
+        middle = j // 2 - last
+        none = (3 - j) // 3
+        first = 1 - last - middle - none
+        return (
+            none * self.z
+            + first * (1 - self.z + 4 * self.high)
+            + middle * (2 - self.high)
+            + last * (3 - 3 * self.high)
+        )
+
+
+def remote(source, target, send_sem, recv_sem, device):
+    return pltpu.make_async_remote_copy(
+        src_ref=source,
+        dst_ref=target,
+        send_sem=send_sem,
+        recv_sem=recv_sem,
+        device_id=device,
+        device_id_type=MESH,
+    )
+
+
+def greet(partners):
+    entry = pltpu.get_barrier_semaphore()
+    for partner in partners:
+        pl.semaphore_signal(entry, inc=1, device_id=partner, device_id_type=MESH)
+    pl.semaphore_wait(entry, len(partners))
+
+
+def exchange_pass(at, held, gather_sems, sum_sems, sum_bufs, part_own, compute):
+    z_own, z_next, z_in, y_out, y_in, c_out, c_in = gather_sems
+    t_out, t_in, v_out, v_in, w_out, w_in = sum_sems
+    to_sib, from_sib, chip_sum, from_y, to_z, from_z = sum_bufs
+    f, core = at.f, at.core
+
+    def block(chip):
+        return held.at[chip, core]
+
+    def over(chip, outgoing, incoming, device):
+        return remote(block(chip), block(chip), outgoing, incoming, device)
+
+    def own_z(step, slot):
+        return over(f, z_own.at[slot], z_in.at[at.z], at.at_z(at.z + step))
+
+    def own_z_toward():
+        return own_z(at.toward, 0)
+
+    def own_z_away():
+        return own_z(-at.toward, 1)
+
+    def pass_z(src, step):
+        return over(src * 2 + at.y, z_next.at[src], z_in.at[src], at.at_z(at.z + step))
+
+    def pass_y(src):
+        return over(src * 2 + at.y, y_out.at[src], y_in.at[src], at.over_y)
+
+    def pass_sib(chip):
+        return over(chip, c_out.at[chip], c_in.at[chip], at.sibling)
+
+    own_z_toward().start()
+
+    @pl.when(at.inner)
+    def _():
+        own_z_away().start()
+
+    pass_y(at.z).start()
+    pass_sib(f).start()
+
+    def from_z_block(src):
+        return over(src * 2 + at.y, z_next.at[src], z_in.at[src], at.at_z(src))
+
+    def take_z(j, step):
+        src = at.source(j)
+        from_z_block(src).wait_recv()
+
+        @pl.when(at.inner)
+        def _():
+            pass_z(src, step).start()
+
+        pass_y(src).start()
+        pass_sib(src * 2 + at.y).start()
+
+    def chip_of(i):
+        return at.source(i // 2) * 2 + lax.rem(at.y + lax.rem(i, 2), 2)
+
+    def sib_sum(i):
+        return remote(to_sib.at[i], from_sib.at[i], t_out.at[i], t_in.at[i], at.sibling)
+
+    def y_sum(i):
+        return remote(chip_sum.at[i], from_y.at[i // 2], v_out.at[i // 2], v_in.at[i // 2], at.over_y)
+
+    def finish_chip(i):
+        sib_sum(i).wait_recv()
+        chip_sum[i] = (part_own[...] + from_sib[i].astype(jnp.float32)).astype(jnp.bfloat16)
+
+    def step(i, carried):
+        side = lax.rem(i, 2)
+        chip = chip_of(i)
+
+        @pl.when(i == 1)
+        def _():
+            take_z(1, at.toward)
+
+            @pl.when(at.inner)
+            def _():
+                take_z(2, -at.toward)
+
+        @pl.when((i == 3) & at.outer)
+        def _():
+            take_z(2, -at.toward)
+
+        @pl.when(i == 5)
+        def _():
+            take_z(3, -at.toward)
+
+        @pl.when(side == 1)
+        def _():
+            pass_y(at.source(i // 2)).wait_recv()
+            pass_sib(chip).start()
+
+        pass_sib(chip).wait_recv()
+        own_part, sib_part = compute(chip)
+        to_sib[i] = sib_part.astype(jnp.bfloat16)
+        sib_sum(i).start()
+
+        @pl.when(i > 0)
+        def _():
+            finish_chip(i - 1)
+
+        part_own[...] = own_part
+
+        @pl.when((side == 0) & (i > 2))
+        def _():
+            y_sum(i - 1).start()
+
+        return carried
+
+    lax.fori_loop(0, 8, step, 0)
+    finish_chip(7)
+    y_sum(7).start()
+    y_sum(1).start()
+
+    def z_sum(j):
+        target = at.source(j)
+        return remote(to_z.at[j - 1], from_z.at[at.z], w_out.at[j - 1], w_in.at[at.z], at.at_z(target))
+
+    def from_z_sum(j):
+        src = at.source(j)
+        return remote(to_z.at[j - 1], from_z.at[src], w_out.at[j - 1], w_in.at[src], at.at_z(src))
+
+    for j in (1, 2, 3):
+        y_sum(2 * j + 1).wait_recv()
+        to_z[j - 1] = (
+            chip_sum[2 * j].astype(jnp.float32) + from_y[j].astype(jnp.float32)
+        ).astype(jnp.bfloat16)
+        z_sum(j).start()
+
+    def finish():
+        y_sum(1).wait_recv()
+        total = chip_sum[0].astype(jnp.float32) + from_y[0].astype(jnp.float32)
+        for j in (1, 2, 3):
+            from_z_sum(j).wait_recv()
+            total = total + from_z[at.source(j)].astype(jnp.float32)
+        return total
+
+    def drain():
+        own_z_toward().wait_send()
+
+        @pl.when(at.inner)
+        def _():
+            own_z_away().wait_send()
+            for j in (1, 2, 3):
+                from_z_block(at.source(j)).wait_send()
+
+        def drain_chip(i, carried):
+            pass_sib(chip_of(i)).wait_send()
+            sib_sum(i).wait_send()
+
+            @pl.when(lax.rem(i, 2) == 1)
+            def _():
+                pass_y(at.source(i // 2)).wait_send()
+                y_sum(i).wait_send()
+
+            return carried
+
+        lax.fori_loop(0, 8, drain_chip, 0)
+        for j in (1, 2, 3):
+            z_sum(j).wait_send()
+
+    return finish, drain
+
+
+def ffn_kernel(
+    normed_ref,
+    middle_ref,
+    cotangent_ref,
+    gain_ref,
+    own_gate,
+    own_up,
+    own_down,
+    peer_gate,
+    peer_up,
+    peer_down,
+    result_ref,
+    back_ref,
+    gain_grad_ref,
+    gate_grad_ref,
+    up_grad_ref,
+    down_grad_ref,
+    normed_all,
+    grad_all,
+    gate_keep,
+    up_keep,
+    peer_sum,
+    part_own,
+    to_sib,
+    from_sib,
+    chip_sum,
+    from_y,
+    to_z,
+    from_z,
+    to_x,
+    from_x,
+    *sems,
+):
+    at = Place()
+    core = at.core
+    fwd_gather, fwd_sum = sems[:7], sems[7:13]
+    bwd_gather, bwd_sum = sems[13:20], sems[20:26]
+    x_out, x_in = sems[26:28]
+    sum_bufs = (to_sib, from_sib, chip_sum, from_y, to_z, from_z)
+    gates, ups, downs = (own_gate, peer_gate), (own_up, peer_up), (own_down, peer_down)
+    normed_all[at.f, core] = normed_ref[...]
+    greet(
+        [at.sibling, at.over_x, at.over_y]
+        + [at.at_z(lax.rem(at.z + step, 4)) for step in (1, 2, 3)]
+    )
+
+    def rows_of(ref, chip):
+        return jnp.concatenate([ref[chip, core], ref[chip, 1 - core]], axis=0)
+
+    def forward(chip):
+        rows = rows_of(normed_all, chip)
+        total = None
+        for half in (0, 1):
+            gate = nt(rows, gates[half][...])
+            up = nt(rows, ups[half][...])
+            gate_keep[half, chip] = gate
+            up_keep[half, chip] = up
+            bend = jnp.tanh(gelu_c * (gate + 0.044715 * gate * gate * gate))
+            hidden = (0.5 * gate * (1.0 + bend) * up).astype(jnp.bfloat16)
+            part = nn(hidden, downs[half][...])
+            total = part if total is None else total + part
+        return total[:128], total[128:]
+
+    finish, drain = exchange_pass(
+        at, normed_all, fwd_gather, fwd_sum, sum_bufs, part_own, forward
+    )
+    ffn_raw = finish()
+    drain()
+    gain = gain_ref[...]
+    scale = lax.rsqrt(jnp.mean(ffn_raw * ffn_raw, axis=1, keepdims=True) + norm_eps)
+    result_ref[...] = (middle_ref[...] + ffn_raw * scale * gain).astype(jnp.bfloat16)
+    upstream = cotangent_ref[...].astype(jnp.float32)
+    weighted = upstream * gain
+    inner = jnp.mean(weighted * ffn_raw, axis=1, keepdims=True)
+    ffn_grad = scale * weighted - ffn_raw * (scale * scale * scale * inner)
+    gain_grad_ref[...] = jnp.sum(upstream * ffn_raw * scale, axis=0, keepdims=True)
+    grad_all[at.f, core] = ffn_grad.astype(jnp.bfloat16)
+
+    grads = ((gate_grad_ref, up_grad_ref, down_grad_ref), tuple(peer_sum.at[k] for k in range(3)))
+    for half in (0, 1):
+        for target in grads[half]:
+            target[...] = jnp.zeros(target.shape, jnp.float32)
+
+    def backward(chip):
+        rows = rows_of(grad_all, chip)
+        ahead = rows_of(normed_all, chip)
+        total = None
+        for half in (0, 1):
+            dhidden = nt(rows, downs[half][...])
+            gate = gate_keep[half, chip]
+            up = up_keep[half, chip]
+            square = gate * gate
+            bend = jnp.tanh(gelu_c * (gate + 0.044715 * square * gate))
+            unit = 0.5 * gate * (1.0 + bend)
+            slope = 0.5 * (1.0 + bend) + 0.5 * gate * (1.0 - bend * bend) * (
+                gelu_c * (1.0 + 3 * 0.044715 * square)
+            )
+            hidden = (unit * up).astype(jnp.bfloat16)
+            dgate = (dhidden * up * slope).astype(jnp.bfloat16)
+            dup = (dhidden * unit).astype(jnp.bfloat16)
+            part = nn(dgate, gates[half][...]) + nn(dup, ups[half][...])
+            total = part if total is None else total + part
+            gate_sum, up_sum, down_sum = grads[half]
+            gate_sum[...] += tn(dgate, ahead)
+            up_sum[...] += tn(dup, ahead)
+            down_sum[...] += tn(hidden, rows)
+        return total[:128], total[128:]
+
+    finish, drain = exchange_pass(
+        at, grad_all, bwd_gather, bwd_sum, sum_bufs, part_own, backward
+    )
+
+    def x_copy(which):
+        return remote(to_x.at[which], from_x.at[which], x_out.at[which], x_in.at[which], at.over_x)
+
+    for which in range(3):
+        to_x[which] = peer_sum[which].astype(jnp.bfloat16)
+        x_copy(which).start()
+    back_ref[...] = finish()
+    drain()
+    for which in range(3):
+        x_copy(which).wait()
+        grads[0][which][...] += from_x[which].astype(jnp.float32)
+
+
+def ffn_both(normed, middle, cotangent, gain, own, peer):
+    rows, width = normed.shape
+    units = own[0].shape[0]
+    b16, f32 = jnp.bfloat16, jnp.float32
+    vmem = pl.BlockSpec(memory_space=pltpu.VMEM)
+    gather_sems = [DMA((2,)), DMA((4,)), DMA((4,)), DMA((4,)), DMA((4,)), DMA((8,)), DMA((8,))]
+    sum_sems = [DMA((8,)), DMA((8,)), DMA((4,)), DMA((4,)), DMA((3,)), DMA((4,))]
+    return pl.pallas_call(
+        ffn_kernel,
+        out_shape=(
+            jax.ShapeDtypeStruct((rows, width), b16),
+            jax.ShapeDtypeStruct((rows, width), f32),
+            jax.ShapeDtypeStruct((1, width), f32),
+            jax.ShapeDtypeStruct((units, width), f32),
+            jax.ShapeDtypeStruct((units, width), f32),
+            jax.ShapeDtypeStruct((units, width), f32),
+        ),
+        in_specs=[vmem] * 10,
+        out_specs=[vmem] * 6,
+        scratch_shapes=[
+            pltpu.VMEM((8, 2, rows, width), b16),
+            pltpu.VMEM((8, 2, rows, width), b16),
+            pltpu.VMEM((2, 8, 2 * rows, units), f32),
+            pltpu.VMEM((2, 8, 2 * rows, units), f32),
+            pltpu.VMEM((3, units, width), f32),
+            pltpu.VMEM((rows, width), f32),
+            pltpu.VMEM((8, rows, width), b16),
+            pltpu.VMEM((8, rows, width), b16),
+            pltpu.VMEM((8, rows, width), b16),
+            pltpu.VMEM((4, rows, width), b16),
+            pltpu.VMEM((3, rows, width), b16),
+            pltpu.VMEM((4, rows, width), b16),
+            pltpu.VMEM((3, units, width), b16),
+            pltpu.VMEM((3, units, width), b16),
+        ]
+        + (gather_sems + sum_sems) * 2
+        + [DMA((3,)), DMA((3,))],
+        compiler_params=pltpu.CompilerParams(
+            collective_id=1, has_side_effects=True, vmem_limit_bytes=62 << 20
+        ),
+        name="ffn_both",
+    )(normed, middle, cotangent, gain, *own, *peer)
+
+
 def gather_rows(block):
     return lax.all_gather(block, ("fsdp", "seq"), axis=0, tiled=True)
 
@@ -329,25 +735,15 @@
     attn_out, post_pull = jax.vjp(scaled_norm, attn_raw, gain_post)
     middle = residual + attn_out
     normed_ffn, pre_ffn_pull = jax.vjp(scaled_norm, middle, gain_pre_ffn)
-    normed_all = gather_rows(normed_ffn.astype(jnp.bfloat16))
-    gate_act = outer_rows(normed_all, w_gate.T)
-    up_act = outer_rows(normed_all, w_up.T)
-    hidden, glu_pull = jax.vjp(gated_unit, gate_act, up_act)
-    hidden_b = hidden.astype(jnp.bfloat16)
-    ffn_raw = scatter_rows(product(hidden_b, w_down))
-    ffn_out, post_ffn_pull = jax.vjp(scaled_norm, ffn_raw, gain_post_ffn)
-    result = (middle + ffn_out).astype(jnp.bfloat16)
+    own_ffn = (w_gate.T, w_up.T, w_down)
+    peer_ffn = tuple(
+        lax.ppermute(block, "seq", [(0, 2), (2, 0), (1, 3), (3, 1)]) for block in own_ffn
+    )
+    result, normed_ffn_grad, gain_post_ffn_grad, gate_w_grad_t, up_w_grad_t, down_grad = ffn_both(
+        normed_ffn.astype(jnp.bfloat16), middle, cotangent, gain_post_ffn[None], own_ffn, peer_ffn
+    )
+    gain_post_ffn_grad = gain_post_ffn_grad[0]
     upstream = cotangent.astype(jnp.float32)
-    ffn_grad, gain_post_ffn_grad = post_ffn_pull(upstream)
-    ffn_grad_all = gather_rows(ffn_grad.astype(jnp.bfloat16))
-    down_grad = inner_rows(hidden_b, ffn_grad_all)
-    hidden_grad = outer_rows(ffn_grad_all, w_down)
-    gate_grad, up_grad = glu_pull(hidden_grad)
-    gate_grad_b = gate_grad.astype(jnp.bfloat16)
-    up_grad_b = up_grad.astype(jnp.bfloat16)
-    gate_w_grad_t = inner_rows(gate_grad_b, normed_all)
-    up_w_grad_t = inner_rows(up_grad_b, normed_all)
-    normed_ffn_grad = scatter_rows(product(gate_grad_b, w_gate.T) + product(up_grad_b, w_up.T))
     middle_part, gain_pre_ffn_grad = pre_ffn_pull(normed_ffn_grad)
     middle_grad = upstream + middle_part
     attn_grad, gain_post_grad = post_pull(middle_grad)
@@ -450,5 +846,5 @@
         P(None, ("fsdp", "seq")),
         P(("fsdp", "seq"), None),
     )
-    body = split_model if mesh.size <= 32 else local
+    body = split_model if dict(mesh.shape) == {"fsdp": 8, "seq": 4} else local
     return jax.shard_map(body, mesh=mesh, in_specs=in_specs, out_specs=out_specs, check_vma=False)

time: 763 us -> 463 us (0.61)
  waiting for transfers between devices: 599 us -> 186 us
  Pallas kernels: 0 us -> 166 us
  matrix products: 89.4 us -> 25.2 us
  local copies, waits for them, and re-layouts: 24.5 us -> 33.1 us
    reduce_scatter x2 -> x0, waiting for transfers between devices: 268 us -> none  [scatter_rows(): lax.psum_scatter(partial_sum.astype(jnp.bfloat16), ('fsdp', 'seq'), scatt...]
    pallas_call x0 -> x1, Pallas kernels: none -> 166 us  [ffn_both(): pl.pallas_call(ffn_kernel, out_shape=(jax.ShapeDtypeStruct((rows, width),...]
    all_gather x3 -> x1, waiting for transfers between devices: 232 us -> 71.2 us  [gather_rows(): return lax.all_gather(block, ('fsdp', 'seq'), axis=0, tiled=True)]
    dot_general x9 -> x6, matrix products: 32 us -> 6.48 us  [product(): return jnp.dot(former, latter, preferred_element_type=jnp.float32)]
    dot_general x9 -> x6, matrix products: 30.4 us -> 7.41 us  [outer_rows(): lax.dot_general(former, latter, (((1,), (1,)), ((), ())), preferred_eleme...]
    unnamed x8 -> x4, waiting for transfers between devices: 89.2 us -> 109 us
    dot_general x9 -> x6, matrix products: 27 us -> 11.3 us  [inner_rows(): lax.dot_general(former, latter, (((0,), (0,)), ((), ())), preferred_eleme...]
    unnamed x153 -> x93, local copies, waits for them, and re-layouts: 11.5 us -> 20.1 us
  transfers between devices with their start and end apart: 7 -> 6, of which waited for: 7 -> 3; matrix products, arithmetic and copies ran while one was open for 4% -> 7% of each run, Pallas kernels for 0% -> 0%
where the time goes in v2:
time: 463 us; the launch traced here: 462 us
  waiting for transfers between devices  186 us (40%)
  Pallas kernels  166 us (36%)
  local copies, waits for them, and re-layouts  33.1 us (7%)
  matrix products  25.2 us (5%)
  other arithmetic  24.2 us (5%)
  between operations  14.5 us (3%)
  blocking collectives  7.2 us (2%)
  starting transfers between devices  5.37 us (1%)
    pallas_call x1, Pallas kernels, ffn_both(): pl.pallas_call(ffn_kernel, out_shape=(jax.ShapeDtypeStruct((rows, width),...  166 us
    unnamed x4, waiting for transfers between devices  109 us
    all_gather x1, waiting for transfers between devices, gather_rows(): return lax.all_gather(block, ('fsdp', 'seq'), axis=0, tiled=True)  71.2 us
    unnamed x93, local copies, waits for them, and re-layouts  20.1 us
    dot_general x6, matrix products, inner_rows(): lax.dot_general(former, latter, (((0,), (0,)), ((), ())), preferred_eleme...  11.3 us
  transfers between devices with their start and end apart: 6, of which 3 were waited for; matrix products, arithmetic and copies ran while one was open for 7% of the time, Pallas kernels for 0%

profile of v2, /device:TPU:0, one launch (start us, length us, event | category | flops | bytes accessed | tf_op | source)
XLA Modules:
  0.0 461.8 jit_solution(11147134841348503857)
XLA Ops:
  11.9 3.0 collective-permute-start
  15.0 1.9 collective-permute-start.2
  19.8 71.2 %all-gather.2.cloned.1.call-done = bf16[2816,1152]{1,0:T(8,128)(2,1)} async-done(((bf16[88,1152]{1,0:T(8,128)(2,1)}), bf16[2816,1152]{1,0:T(8,128)(2,1)}) %all-gather.2.cloned.1.call-update) | async-done | bytes 6488080 | tf_op jit(solution)/shard_map/all_gather | solution.py:668
  92.1 1.6 multiply_reduce_fusion.10
  93.8 1.5 convolution_convert_fusion.7
  95.3 2.8 fusion.70
  99.3 7.2 %all_gather.7 = bf16[512,512]{1,0:T(8,128)(2,1)S(1)} all-gather(bf16[128,512]{1,0:T(8,128)(2,1)S(1)} %pad_maximum_fusion.2), channel_id=1, replica_groups=mesh['fsdp'=8,'seq'=4] {'seq'}, dimensions={0}, use_global_device_ids=true | all-gather | bytes 655360 | tf_op jit(solution)/shard_map/all_gather | solution.py:716
  113.3 165.8 %ffn_both.1 = (bf16[128,1152]{1,0:T(8,128)(2,1)}, f32[128,1152]{1,0:T(8,128)}, f32[1,1152]{1,0:T(1,128)}, f32[216,1152]{1,0:T(8,128)}, f32[216,1152]{1,0:T(8,128)}, /*index=5*/f32[216,1152]{1,0:T(8,128)}) custom-call(bf16[128,1152]{1,0:T(8,128)(2,1)} %multiply_convert_fusion.1.normed_ref, f32[128,1152]{1,0:T(8,128)} %copy-done.3, ...), custom_call_target="tpu_custom_call" | custom-call | tf_op jit(solution)/shard_map/ffn_both/pallas_call | solution.py:630
  279.2 2.1 multiply_reduce_fusion.1
  281.3 2.3 multiply_reduce_fusion.2
  284.6 2.5 convolution_convert_fusion.5
  294.8 1.6 fusion.18
  298.8 2.9 fusion.1
  301.7 3.1 fusion
  304.9 1.5 fusion.74
  306.4 6.7 %reduce-scatter.5.cloned.1.call-done = bf16[128,512]{1,0:T(8,128)(2,1)} async-done(((bf16[512,512]{1,0:T(8,128)(2,1)}), bf16[128,512]{1,0:T(8,128)(2,1)}) %reduce-scatter.5.cloned.1.call-update) | async-done | bytes 131088 | tf_op jit(solution)/shard_map/reduce_scatter | solution.py:764
  319.0 1.5 fusion.12
  320.5 1.5 dynamic-update-slice.5
  330.0 1.9 fusion.2
  331.9 2.1 fusion.4
  335.9 108.5 %reduce-scatter.7.cloned.1.call-done = bf16[88,1152]{1,0:T(8,128)(2,1)} async-done(((bf16[2816,1152]{1,0:T(8,128)(2,1)}), bf16[88,1152]{1,0:T(8,128)(2,1)}) %reduce-scatter.7.cloned.1.call-update) | async-done | bytes 202768
  446.6 1.6 slice.121
  449.4 1.7 copy.63
  451.1 2.2 copy.64
  (165 shorter events, 48.6 us)
Async XLA Ops:
  7.2 83.8 %all-gather.2.cloned.1.call-start = ((), (), s32[]{:S(2)}) async-start(), calls=%async_computation.2 | async-start | bytes 6690816 | tf_op jit(solution)/shard_map/all_gather | solution.py:668
  11.8 301.2 %reduce-scatter.5.cloned.1.call-start = ((), (), s32[]{:S(2)}) async-start(), calls=%async_computation.3 | async-start | bytes 655360 | tf_op jit(solution)/shard_map/reduce_scatter | solution.py:764
  11.9 101.4 %collective-permute-start = (bf16[216,1152]{1,0:T(8,128)(2,1)}, bf16[216,1152]{1,0:T(8,128)(2,1)}, u32[]{:S(2)}, u32[]{:S(2)}) collective-permute-start(bf16[216,1152]{1,0:T(8,128)(2,1)} %bitcast.142), channel_id=1, source_target_pairs={{0,2},{2,0},{1,3},{3,1},{4,6},{6,4},{5,7},{7,5},{8,10},{10,8},{9,1... | collective-permute-start | bytes 1493000 | tf_op jit(solution)/shard_map/ppermute | solution.py:740
  14.9 98.4 %collective-permute-start.1 = (bf16[216,1152]{1,0:T(8,128)(2,1)}, bf16[216,1152]{1,0:T(8,128)(2,1)}, u32[]{:S(2)}, u32[]{:S(2)}) collective-permute-start(bf16[216,1152]{1,0:T(8,128)(2,1)} %bitcast.144), channel_id=1, source_target_pairs={{0,2},{2,0},{1,3},{3,1},{4,6},{6,4},{5,7},{7,5},{8,10},{10,8},{9,1... | collective-permute-start | bytes 1493000 | tf_op jit(solution)/shard_map/ppermute | solution.py:740
  15.0 98.3 %collective-permute-start.2 = (bf16[216,1152]{1,0:T(8,128)(2,1)}, bf16[216,1152]{1,0:T(8,128)(2,1)}, u32[]{:S(2)}, u32[]{:S(2)}) collective-permute-start(bf16[216,1152]{1,0:T(8,128)(2,1)} %own_down.1), channel_id=1, source_target_pairs={{0,2},{2,0},{1,3},{3,1},{4,6},{6,4},{5,7},{7,5},{8,10},{10,8},{9,1... | collective-permute-start | bytes 1493000 | tf_op jit(solution)/shard_map/ppermute | solution.py:740
  16.9 82.0 %copy-start.33 = (f32[128]{0:T(128)}, f32[128]{0:T(128)S(1)}, u32[]{:S(2)}) copy-start(f32[128]{0:T(128)S(1)} %multiply_power_fusion) | copy-start | bytes 1540
  18.0 73.0 %copy-start.35 = (f32[128]{0:T(128)}, f32[128]{0:T(128)S(1)}, u32[]{:S(2)}) copy-start(f32[128]{0:T(128)S(1)} %fusion.16) | copy-start | bytes 1540
  18.1 88.5 %copy-start.31 = (f32[128]{0:T(128)}, f32[128]{0:T(128)S(1)}, u32[]{:S(2)}) copy-start(f32[128]{0:T(128)S(1)} %fusion.57) | copy-start | bytes 1540
  18.7 80.5 %copy-start.28 = (f32[128]{0:T(128)}, f32[128]{0:T(128)S(1)}, u32[]{:S(2)}) copy-start(f32[128]{0:T(128)S(1)} %get-tuple-element.66) | copy-start | bytes 1540
  19.8 88.7 %copy-start.16 = (f32[128,128]{1,0:T(8,128)}, f32[128,128]{1,0:T(8,128)S(1)}, u32[]{:S(2)}) copy-start(f32[128,128]{1,0:T(8,128)S(1)} %get-tuple-element.53) | copy-start | bytes 196612
  19.8 88.7 %copy-start.18 = (f32[128,128]{1,0:T(8,128)}, f32[128,128]{1,0:T(8,128)S(1)}, u32[]{:S(2)}) copy-start(f32[128,128]{1,0:T(8,128)S(1)} %get-tuple-element.54) | copy-start | bytes 196612
  92.1 15.4 %copy-start.27 = (f32[256]{0:T(256)}, f32[256]{0:T(256)S(1)}, u32[]{:S(2)}) copy-start(f32[256]{0:T(256)S(1)} %get-tuple-element.51) | copy-start | bytes 3076
  109.3 177.9 %copy-start.29 = (f32[512]{0:T(512)}, f32[512]{0:T(512)S(1)}, u32[]{:S(2)}) copy-start(f32[512]{0:T(512)S(1)} %get-tuple-element.59) | copy-start | bytes 6148
  110.3 176.9 %copy-start.30 = (f32[512]{0:T(512)}, f32[512]{0:T(512)S(1)}, u32[]{:S(2)}) copy-start(f32[512]{0:T(512)S(1)} %fusion.8) | copy-start | bytes 6148
  110.9 172.7 %copy-start.11 = (bf16[4,128,256]{1,2,0:T(8,128)(2,1)}, bf16[4,128,256]{1,2,0:T(8,128)(2,1)S(1)}, u32[]{:S(2)}) copy-start(bf16[4,128,256]{1,2,0:T(8,128)(2,1)S(1)} %copy.31) | copy-start | bytes 786436
  112.5 171.1 %copy-start.38 = (f32[128]{0:T(128)S(1)}, f32[128]{0:T(128)}, u32[]{:S(2)}) copy-start(f32[128]{0:T(128)} %copy-done.37) | copy-start | bytes 1540
  291.9 152.4 %reduce-scatter.7.cloned.1.call-start = ((), (), s32[]{:S(2)}) async-start(), calls=%async_computation.4 | async-start | bytes 6690816
  298.8 26.0 %copy-start.26 = (bf16[1152]{0:T(1024)(128)(2,1)S(1)}, bf16[1152]{0:T(1024)(128)(2,1)}, u32[]{:S(2)}) copy-start(bf16[1152]{0:T(1024)(128)(2,1)} %get-tuple-element.24) | copy-start | bytes 6916
  298.8 27.4 %copy-start.25 = (bf16[1152]{0:T(1024)(128)(2,1)S(1)}, bf16[1152]{0:T(1024)(128)(2,1)}, u32[]{:S(2)}) copy-start(bf16[1152]{0:T(1024)(128)(2,1)} %get-tuple-element.22) | copy-start | bytes 6916
  317.6 17.3 %copy-start.8 = (f32[128,1152]{1,0:T(8,128)S(1)}, f32[128,1152]{1,0:T(8,128)}, u32[]{:S(2)}) copy-start(f32[128,1152]{1,0:T(8,128)} %copy-done.7) | copy-start | bytes 1769476
  319.0 15.9 %copy-start.36 = (f32[128]{0:T(128)S(1)}, f32[128]{0:T(128)}, u32[]{:S(2)}) copy-start(f32[128]{0:T(128)} %copy-done.35) | copy-start | bytes 1540
  319.0 15.9 %copy-start.32 = (f32[128]{0:T(128)S(1)}, f32[128]{0:T(128)}, u32[]{:S(2)}) copy-start(f32[128]{0:T(128)} %copy-done.31) | copy-start | bytes 1540
  333.9 119.4 %copy-start.15 = (f32[216,1152]{1,0:T(8,128)S(1)}, f32[216,1152]{1,0:T(8,128)}, u32[]{:S(2)}) copy-start(f32[216,1152]{1,0:T(8,128)} %get-tuple-element.20) | copy-start | bytes 2985988
  334.8 119.5 %copy-start.14 = (f32[216,1152]{1,0:T(8,128)S(1)}, f32[216,1152]{1,0:T(8,128)}, u32[]{:S(2)}) copy-start(f32[216,1152]{1,0:T(8,128)} %get-tuple-element.87) | copy-start | bytes 2985988
  (22 other events, 127.4 us)
Sparse Core Ops, SparseCore 0:
  12.0 78.9 all-gather.1
  292.1 20.9 reduce-scatter.4
  335.0 109.3 reduce-scatter.6

commit v3 on v0

--- a/solution.py
+++ b/solution.py
@@ -3,6 +3,8 @@
 import jax
 import jax.numpy as jnp
 from jax import lax
+from jax.experimental import pallas as pl
+from jax.experimental.pallas import tpu as pltpu
 from jax.sharding import PartitionSpec as P
 
 norm_eps = 1e-06
@@ -258,6 +260,1212 @@
     )
 
 
+gelu_c = 0.7978845608028654
+MESH = pl.DeviceIdType.MESH
+DMA = pltpu.SemaphoreType.DMA
+
+
+def nt(former, latter):
+    return lax.dot_general(
+        former, latter, (((1,), (1,)), ((), ())), preferred_element_type=jnp.float32
+    )
+
+
+def nn(former, latter):
+    return lax.dot_general(
+        former, latter, (((1,), (0,)), ((), ())), preferred_element_type=jnp.float32
+    )
+
+
+def tn(former, latter):
+    return lax.dot_general(
+        former, latter, (((0,), (0,)), ((), ())), preferred_element_type=jnp.float32
+    )
+
+
+class Place:
+    def __init__(self):
+        self.f = lax.axis_index("fsdp")
+        self.s = lax.axis_index("seq")
+        self.z = self.f // 2
+        self.y = lax.rem(self.f, 2)
+        self.core = lax.rem(self.s, 2)
+        self.high = self.z // 2
+        self.inner = self.z * (3 - self.z) == 2
+        self.outer = self.z * (3 - self.z) == 0
+        self.sibling = (self.f, self.s + 1 - 2 * self.core)
+        self.over_x = (self.f, lax.rem(self.s + 2, 4))
+        self.over_y = (self.f + 1 - 2 * self.y, self.s)
+        self.toward = 1 - 2 * self.high
+        self.step_first = self.toward * (1 - self.z * (3 - self.z))
+
+    def at_z(self, z):
+        return (z * 2 + self.y, self.s)
+
+    def source(self, j):
+        last = j // 3
+        middle = j // 2 - last
+        none = (3 - j) // 3
+        first = 1 - last - middle - none
+        return (
+            none * self.z
+            + first * (1 - self.z + 4 * self.high)
+            + middle * (2 - self.high)
+            + last * (3 - 3 * self.high)
+        )
+
+
+def remote(source, target, send_sem, recv_sem, device):
+    return pltpu.make_async_remote_copy(
+        src_ref=source,
+        dst_ref=target,
+        send_sem=send_sem,
+        recv_sem=recv_sem,
+        device_id=device,
+        device_id_type=MESH,
+    )
+
+
+def greet(partners):
+    entry = pltpu.get_barrier_semaphore()
+    for partner in partners:
+        pl.semaphore_signal(entry, inc=1, device_id=partner, device_id_type=MESH)
+    pl.semaphore_wait(entry, len(partners))
+
+
+def exchange_pass(at, held, gather_sems, sum_sems, sum_bufs, part_own, compute, lag=0, ready=None, then=None):
+    z_own, z_next, z_in, y_out, y_in, c_out, c_in = gather_sems
+    t_out, t_in, v_out, v_in, w_out, w_in = sum_sems
+    to_sib, from_sib, chip_sum, from_y, to_z, from_z = sum_bufs
+    f, core = at.f, at.core
+
+    def block(chip):
+        return held.at[chip, core]
+
+    def over(chip, outgoing, incoming, device):
+        return remote(block(chip), block(chip), outgoing, incoming, device)
+
+    def own_z(step, slot):
+        return over(f, z_own.at[slot], z_in.at[at.z], at.at_z(at.z + step))
+
+    def own_z_toward():
+        return own_z(at.toward, 0)
+
+    def own_z_away():
+        return own_z(-at.toward, 1)
+
+    def pass_z(src, step):
+        return over(src * 2 + at.y, z_next.at[src], z_in.at[src], at.at_z(at.z + step))
+
+    def pass_y(src):
+        return over(src * 2 + at.y, y_out.at[src], y_in.at[src], at.over_y)
+
+    def pass_sib(chip):
+        return over(chip, c_out.at[chip], c_in.at[chip], at.sibling)
+
+    own_z_toward().start()
+
+    @pl.when(at.inner)
+    def _():
+        own_z_away().start()
+
+    pass_y(at.z).start()
+    pass_sib(f).start()
+
+    def from_z_block(src):
+        return over(src * 2 + at.y, z_next.at[src], z_in.at[src], at.at_z(src))
+
+    def take_z(j, step):
+        src = at.source(j)
+        from_z_block(src).wait_recv()
+
+        @pl.when(at.inner)
+        def _():
+            pass_z(src, step).start()
+
+        pass_y(src).start()
+        pass_sib(src * 2 + at.y).start()
+
+    def chip_of(i):
+        return at.source(i // 2) * 2 + lax.rem(at.y + lax.rem(i, 2), 2)
+
+    def sib_sum(i):
+        return remote(to_sib.at[i], from_sib.at[i], t_out.at[i], t_in.at[i], at.sibling)
+
+    def y_sum(i):
+        return remote(chip_sum.at[i], from_y.at[i // 2], v_out.at[i // 2], v_in.at[i // 2], at.over_y)
+
+    def finish_chip(i):
+        sib_sum(i).wait_recv()
+        chip_sum[i] = (part_own[...] + from_sib[i].astype(jnp.float32)).astype(jnp.bfloat16)
+
+    def arrivals(i):
+        @pl.when(i == 1)
+        def _():
+            take_z(1, at.toward)
+
+            @pl.when(at.inner)
+            def _():
+                take_z(2, -at.toward)
+
+        @pl.when((i == 3) & at.outer)
+        def _():
+            take_z(2, -at.toward)
+
+        @pl.when(((i == 3) & at.inner) | ((i == 5) & at.outer))
+        def _():
+            take_z(3, -at.toward)
+
+        @pl.when(lax.rem(i, 2) == 1)
+        def _():
+            pass_y(at.source(i // 2)).wait_recv()
+            pass_sib(chip_of(i)).start()
+
+    def one_chip(i):
+        chip = chip_of(i)
+        pass_sib(chip).wait_recv()
+        own_part, sib_part = compute(chip)
+        to_sib[i] = sib_part.astype(jnp.bfloat16)
+        sib_sum(i).start()
+
+        @pl.when(i > 0)
+        def _():
+            finish_chip(i - 1)
+
+        part_own[...] = own_part
+
+    def step(i, carried):
+        @pl.when(i < 8)
+        def _():
+            arrivals(i)
+
+        if ready is not None:
+
+            @pl.when(i == lag)
+            def _():
+                ready()
+
+        @pl.when(i >= lag)
+        def _():
+            one_chip(i - lag)
+
+        return carried
+
+    lax.fori_loop(0, 8 + lag, step, 0)
+    finish_chip(7)
+    for j in (3, 2, 1, 0):
+        y_sum(2 * j + 1).start()
+    if then is not None:
+        then()
+
+    def z_sum(target, direction):
+        slot = (direction + 1) // 2
+        return remote(
+            to_z.at[target],
+            from_z.at[slot, target],
+            w_out.at[target],
+            w_in.at[slot, target],
+            at.at_z(at.z + direction),
+        )
+
+    def z_arrival(target, direction):
+        slot = (direction + 1) // 2
+        return remote(
+            to_z.at[target],
+            from_z.at[slot, target],
+            w_out.at[target],
+            w_in.at[slot, target],
+            at.at_z(lax.rem(at.z - direction + 4, 4)),
+        )
+
+    def direction_of(j):
+        return at.step_first if j == 1 else at.toward
+
+    for j in (3, 2, 1):
+        target, direction = at.source(j), direction_of(j)
+        y_sum(2 * j + 1).wait_recv()
+        mine = chip_sum[2 * j].astype(jnp.float32) + from_y[j].astype(jnp.float32)
+
+        @pl.when(at.outer)
+        def _():
+            to_z[target] = mine.astype(jnp.bfloat16)
+
+        @pl.when(at.inner)
+        def _():
+            z_arrival(target, direction).wait_recv()
+            ahead = from_z[(direction + 1) // 2, target].astype(jnp.float32)
+            to_z[target] = (mine + ahead).astype(jnp.bfloat16)
+
+        z_sum(target, direction).start()
+
+    def finish():
+        y_sum(1).wait_recv()
+        part_own[...] = chip_sum[0].astype(jnp.float32) + from_y[0].astype(jnp.float32)
+        z_arrival(at.z, -at.toward).wait_recv()
+        part_own[...] += from_z[(1 - at.toward) // 2, at.z].astype(jnp.float32)
+
+        @pl.when(at.inner)
+        def _():
+            z_arrival(at.z, at.toward).wait_recv()
+            part_own[...] += from_z[(1 + at.toward) // 2, at.z].astype(jnp.float32)
+
+        return part_own[...]
+
+    def drain():
+        own_z_toward().wait_send()
+
+        @pl.when(at.inner)
+        def _():
+            own_z_away().wait_send()
+            for j in (1, 2, 3):
+                from_z_block(at.source(j)).wait_send()
+
+        def drain_chip(i, carried):
+            pass_sib(chip_of(i)).wait_send()
+            sib_sum(i).wait_send()
+
+            @pl.when(lax.rem(i, 2) == 1)
+            def _():
+                pass_y(at.source(i // 2)).wait_send()
+                y_sum(i).wait_send()
+
+            return carried
+
+        lax.fori_loop(0, 8, drain_chip, 0)
+        for j in (1, 2, 3):
+            z_sum(at.source(j), direction_of(j)).wait_send()
+
+    return finish, drain
+
+
+gain_edges = (0, 1152, 1408, 1664, 2816, 3968, 5120)
+score_step = 0.0625
+hidden_score = -1e30
+
+
+def shape_spec(shape, dtype):
+    return jax.ShapeDtypeStruct(shape, dtype)
+
+
+def rms_scale(values):
+    return lax.rsqrt(jnp.mean(values * values, axis=-1, keepdims=True) + norm_eps)
+
+
+def norm_back(values, gain, upstream):
+    scale = rms_scale(values)
+    weighted = upstream * gain
+    inner = jnp.mean(weighted * values, axis=-1, keepdims=True)
+    back = scale * weighted - values * (scale * scale * scale * inner)
+    return back, jnp.sum(upstream * values * scale, axis=0, keepdims=True)
+
+
+def pick(offset):
+    row = lax.broadcasted_iota(jnp.int32, (256, 512), 0)
+    column = lax.broadcasted_iota(jnp.int32, (256, 512), 1)
+    wanted = row // 8 * 16 + lax.rem(row, 8) + offset
+    return jnp.where(column == wanted, 1.0, 0.0).astype(jnp.bfloat16)
+
+
+def rows_of_all(w_all, low, count):
+    return jnp.concatenate(
+        [w_all[d // 2, d % 2, low : low + count] for d in range(32)], axis=0
+    )
+
+
+def rows_of_head(w_all, head, low, count):
+    return jnp.concatenate(
+        [w_all[d // 2, d % 2, low : low + count] for d in range(8 * head, 8 * head + 8)], axis=0
+    )
+
+
+class GainGather:
+    def __init__(self, at, held, sems):
+        self.at, self.held = at, held
+        self.out, self.inc, self.z_out, self.z_in = sems
+        x = at.s // 2
+        self.spans = (
+            (at.f * 4 + at.s, 1, at.sibling),
+            (at.f * 4 + 2 * x, 2, at.over_x),
+            (at.f * 4, 4, at.over_y),
+        )
+
+    def stage(self, k):
+        first, count, partner = self.spans[k]
+        span = self.held.at[pl.ds(first, count)]
+        return remote(span, span, self.out.at[k], self.inc.at[k], partner)
+
+    def last(self, src, j, device):
+        span = self.held.at[pl.ds(src * 8, 8)]
+        return remote(span, span, self.z_out.at[j], self.z_in.at[src], device)
+
+    def run(self):
+        at = self.at
+        for k in range(3):
+            self.stage(k).start()
+            self.stage(k).wait_recv()
+        for j in (1, 2, 3):
+            self.last(at.z, j, at.at_z(at.source(j))).start()
+        for j in (1, 2, 3):
+            self.last(at.source(j), j, at.at_z(at.source(j))).wait_recv()
+
+    def drain(self):
+        at = self.at
+        for k in range(3):
+            self.stage(k).wait_send()
+        for j in (1, 2, 3):
+            self.last(at.z, j, at.at_z(at.source(j))).wait_send()
+
+
+class WeightGather:
+    def __init__(self, at, w_all, sems, part, low, middle, high):
+        self.at, self.w_all, self.part = at, w_all, part
+        (
+            self.z_own,
+            self.z_next,
+            self.z_in,
+            self.yf_out,
+            self.yf_in,
+            self.xf_out,
+            self.xf_in,
+            self.yh_out,
+            self.yh_in,
+            self.xh_out,
+            self.xh_in,
+            self.s_out,
+            self.s_in,
+        ) = sems
+        self.low, self.middle, self.high = low, middle, high
+        self.x = at.s // 2
+
+    def block(self, z, y, x, low, high):
+        chip = (z * 2 + y) * 2 + x
+        return self.w_all.at[chip, self.at.core, pl.ds(low, high - low)]
+
+    def whole(self, z, outgoing, incoming, device):
+        span = self.block(z, self.at.y, self.x, self.low, self.high)
+        return remote(span, span, outgoing, incoming, device)
+
+    def own(self, step, slot):
+        at, p = self.at, self.part
+        return self.whole(at.z, self.z_own.at[p, slot], self.z_in.at[p, at.z], at.at_z(at.z + step))
+
+    def passed(self, src, device):
+        p = self.part
+        return self.whole(src, self.z_next.at[p, src], self.z_in.at[p, src], device)
+
+    def y_full(self, src):
+        p = self.part
+        return self.whole(src, self.yf_out.at[p, src], self.yf_in.at[p, src], self.at.over_y)
+
+    def x_full(self, src):
+        p = self.part
+        return self.whole(src, self.xf_out.at[p, src], self.xf_in.at[p, src], self.at.over_x)
+
+    def x_half(self, src):
+        span = self.block(src, 1 - self.at.y, self.x, self.low, self.middle)
+        p = self.part
+        return remote(span, span, self.xh_out.at[p, src], self.xh_in.at[p, src], self.at.over_x)
+
+    def y_half(self, src):
+        span = self.block(src, self.at.y, 1 - self.x, self.middle, self.high)
+        p = self.part
+        return remote(span, span, self.yh_out.at[p, src], self.yh_in.at[p, src], self.at.over_y)
+
+    def sib(self, src):
+        span = self.w_all.at[
+            pl.ds(src * 4, 4), self.at.core, pl.ds(self.low, self.high - self.low)
+        ]
+        p = self.part
+        return remote(span, span, self.s_out.at[p, src], self.s_in.at[p, src], self.at.sibling)
+
+    def begin(self):
+        at = self.at
+        self.own(at.toward, 0).start()
+
+        @pl.when(at.inner)
+        def _():
+            self.own(-at.toward, 1).start()
+
+        self.y_full(at.z).start()
+        self.x_full(at.z).start()
+
+    def take(self, j):
+        at = self.at
+        src = at.source(j)
+        self.passed(src, at.at_z(src)).wait_recv()
+
+        @pl.when(at.inner)
+        def _():
+            self.passed(src, at.at_z(at.z + (at.toward if j == 1 else -at.toward))).start()
+
+        self.y_full(src).start()
+        self.x_full(src).start()
+
+    def cross(self, j):
+        src = self.at.source(j)
+        self.y_full(src).wait_recv()
+        self.x_half(src).start()
+        self.x_full(src).wait_recv()
+        self.y_half(src).start()
+
+    def close(self, j):
+        src = self.at.source(j)
+        self.x_half(src).wait_recv()
+        self.y_half(src).wait_recv()
+        self.sib(src).start()
+
+    def first_half(self):
+        at = self.at
+        self.take(1)
+
+        @pl.when(at.inner)
+        def _():
+            self.take(2)
+
+        self.cross(0)
+
+        @pl.when(at.inner)
+        def _():
+            self.take(3)
+
+        @pl.when(at.outer)
+        def _():
+            self.take(2)
+
+        self.cross(1)
+        self.close(0)
+
+    def second_half(self):
+        @pl.when(self.at.outer)
+        def _():
+            self.take(3)
+
+        self.cross(2)
+        self.close(1)
+        self.cross(3)
+        self.close(2)
+        self.close(3)
+
+    def settle(self):
+        for j in range(4):
+            self.sib(self.at.source(j)).wait_recv()
+
+    def drain(self):
+        at = self.at
+        self.own(at.toward, 0).wait_send()
+
+        @pl.when(at.inner)
+        def _():
+            self.own(-at.toward, 1).wait_send()
+            for j in (1, 2, 3):
+                self.passed(at.source(j), at.at_z(at.source(j))).wait_send()
+
+        for j in range(4):
+            src = at.source(j)
+            for copy in (self.y_full, self.x_full, self.x_half, self.y_half, self.sib):
+                copy(src).wait_send()
+
+
+def gather_weight_sems():
+    return [DMA((2, 2))] + [DMA((2, 4))] * 12
+
+
+def gain_sems():
+    return [DMA((3,)), DMA((3,)), DMA((4,)), DMA((4,))]
+
+
+def turn(values, cos, sin):
+    a, b = values[:, :128], values[:, 128:]
+    return jnp.concatenate([a * cos - b * sin, b * cos + a * sin], axis=1)
+
+
+def turn_back(values, cos, sin):
+    a, b = values[:, :128], values[:, 128:]
+    return jnp.concatenate([a * cos + b * sin, b * cos - a * sin], axis=1)
+
+
+class WeightReturn:
+    def __init__(self, at, held, bufs, sems, part, low, middle, high):
+        self.at, self.held, self.part = at, held, part
+        self.sib_in, self.xh_in, self.yh_in, self.xf_in, self.yf_in, self.z_in = bufs
+        (
+            self.so,
+            self.si,
+            self.xho,
+            self.xhi,
+            self.yho,
+            self.yhi,
+            self.xfo,
+            self.xfi,
+            self.yfo,
+            self.yfi,
+            self.zo,
+            self.zi,
+        ) = sems
+        self.low, self.middle, self.high = low, middle, high
+        self.x = at.s // 2
+        self.rows = pl.ds(low, high - low)
+        self.top = pl.ds(low, middle - low)
+        self.bottom = pl.ds(middle, high - middle)
+
+    def mine(self, z, y, x, rows):
+        return self.held.at[self.at.core, z * 2 + y, x, rows]
+
+    def sib(self, z):
+        pair = pl.ds(z * 2, 2)
+        p = self.part
+        return remote(
+            self.held.at[1 - self.at.core, pair, :, self.rows],
+            self.sib_in.at[pair, :, self.rows],
+            self.so.at[p, z],
+            self.si.at[p, z],
+            self.at.sibling,
+        )
+
+    def x_half(self, z):
+        p = self.part
+        source = self.mine(z, 1 - self.at.y, 1 - self.x, self.top)
+        return remote(
+            source, self.xh_in.at[z, self.top], self.xho.at[p, z], self.xhi.at[p, z], self.at.over_x
+        )
+
+    def y_half(self, z):
+        p = self.part
+        source = self.mine(z, 1 - self.at.y, 1 - self.x, self.bottom)
+        return remote(
+            source,
+            self.yh_in.at[z, self.bottom],
+            self.yho.at[p, z],
+            self.yhi.at[p, z],
+            self.at.over_y,
+        )
+
+    def x_full(self, z):
+        p = self.part
+        source = self.mine(z, self.at.y, 1 - self.x, self.rows)
+        return remote(
+            source,
+            self.xf_in.at[z, self.rows],
+            self.xfo.at[p, z],
+            self.xfi.at[p, z],
+            self.at.over_x,
+        )
+
+    def y_full(self, z):
+        p = self.part
+        source = self.mine(z, 1 - self.at.y, self.x, self.rows)
+        return remote(
+            source,
+            self.yf_in.at[z, self.rows],
+            self.yfo.at[p, z],
+            self.yfi.at[p, z],
+            self.at.over_y,
+        )
+
+    def z_part(self, z):
+        p = self.part
+        source = self.mine(z, self.at.y, self.x, self.rows)
+        return remote(
+            source,
+            self.z_in.at[self.at.z, self.rows],
+            self.zo.at[p, z],
+            self.zi.at[p, self.at.z],
+            self.at.at_z(z),
+        )
+
+    def z_arrival(self, z):
+        p = self.part
+        source = self.mine(z, self.at.y, self.x, self.rows)
+        return remote(
+            source,
+            self.z_in.at[z, self.rows],
+            self.zo.at[p, z],
+            self.zi.at[p, z],
+            self.at.at_z(z),
+        )
+
+    def add(self, z, y, x, rows, more):
+        core, f = self.at.core, z * 2 + y
+        self.held[core, f, x, rows] = (
+            self.held[core, f, x, rows].astype(jnp.float32) + more.astype(jnp.float32)
+        ).astype(jnp.bfloat16)
+
+    def send_sib(self):
+        for j in (3, 2, 1, 0):
+            self.sib(self.at.source(j)).start()
+
+    def merge(self):
+        for j in (3, 2, 1, 0):
+            z = self.at.source(j)
+            self.sib(z).wait_recv()
+            for y in (0, 1):
+                for x in (0, 1):
+                    self.add(z, y, x, self.rows, self.sib_in[z * 2 + y, x, self.rows])
+            self.x_half(z).start()
+            self.y_half(z).start()
+
+    def pair_up(self):
+        at = self.at
+        for j in (3, 2, 1, 0):
+            z = at.source(j)
+            self.x_half(z).wait_recv()
+            self.add(z, 1 - at.y, self.x, self.top, self.xh_in[z, self.top])
+            self.y_full(z).start()
+            self.y_half(z).wait_recv()
+            self.add(z, at.y, 1 - self.x, self.bottom, self.yh_in[z, self.bottom])
+            self.x_full(z).start()
+
+    def collect(self):
+        at = self.at
+        for j in (3, 2, 1, 0):
+            z = at.source(j)
+            self.y_full(z).wait_recv()
+            self.x_full(z).wait_recv()
+            more = self.yf_in[z, self.rows].astype(jnp.float32) + self.xf_in[
+                z, self.rows
+            ].astype(jnp.float32)
+            self.add(z, at.y, self.x, self.rows, more)
+            if j > 0:
+                self.z_part(z).start()
+
+    def total(self):
+        at = self.at
+        value = self.held[at.core, at.f, self.x, self.rows].astype(jnp.float32)
+        for j in (3, 2, 1):
+            z = at.source(j)
+            self.z_arrival(z).wait_recv()
+            value = value + self.z_in[z, self.rows].astype(jnp.float32)
+        return value
+
+    def drain(self):
+        for j in range(4):
+            z = self.at.source(j)
+            for copy in (self.sib, self.x_half, self.y_half, self.x_full, self.y_full):
+                copy(z).wait_send()
+            if j > 0:
+                self.z_part(z).wait_send()
+
+
+class GainSum:
+    def __init__(self, at, row, outgoing, incoming, sems):
+        self.at, self.row, self.outgoing, self.incoming = at, row, outgoing, incoming
+        self.out, self.inc = sems
+        self.partners = (at.sibling, at.over_x, at.over_y)
+
+    def stage(self, k):
+        return remote(
+            self.outgoing.at[k],
+            self.incoming.at[k],
+            self.out.at[k],
+            self.inc.at[k],
+            self.partners[k],
+        )
+
+    def last(self, src, j, device):
+        return remote(
+            self.outgoing.at[3],
+            self.incoming.at[3 + src],
+            self.out.at[2 + j],
+            self.inc.at[3 + src],
+            device,
+        )
+
+    def send(self, k):
+        self.outgoing[k] = self.row[...]
+        if k < 3:
+            self.stage(k).start()
+        else:
+            for j in (1, 2, 3):
+                self.last(self.at.z, j, self.at.at_z(self.at.source(j))).start()
+
+    def take(self, k):
+        if k < 3:
+            self.stage(k).wait_recv()
+            self.row[...] += self.incoming[k]
+        else:
+            for j in (1, 2, 3):
+                src = self.at.source(j)
+                self.last(src, j, self.at.at_z(src)).wait_recv()
+                self.row[...] += self.incoming[3 + src]
+
+    def drain(self):
+        for k in range(3):
+            self.stage(k).wait_send()
+        for j in (1, 2, 3):
+            self.last(self.at.z, j, self.at.at_z(self.at.source(j))).wait_send()
+
+
+class Refs:
+    def __init__(self, names, refs):
+        for name, ref in zip(names, refs):
+            setattr(self, name, ref)
+
+
+def columns_of(head):
+    return slice(256 * head, 256 * head + 256)
+
+
+def front_phase(at, r, sems):
+    core, s = at.core, at.s
+    gathered = GainGather(at, r.gain_all, sems[:4])
+    w_sems = sems[4:17]
+    kv_out, kv_in, x_out, x_in = sems[17:21]
+    w_all, kv_all = r.w_all, r.kv_all
+    early = WeightGather(at, w_all, w_sems, 0, 0, 16, 48)
+    late = WeightGather(at, w_all, w_sems, 1, 48, 64, 80)
+    chip = at.f * 2 + s // 2
+    w_all[chip, core, 0:32] = r.own_q[...]
+    w_all[chip, core, 32:48] = jnp.concatenate(
+        [r.own_k[...].astype(jnp.float32), r.own_v[...].astype(jnp.float32)], axis=0
+    ).astype(jnp.bfloat16)
+    w_all[chip, core, 48:80] = r.own_o[...]
+    r.gain_all[at.f * 4 + s] = r.gain_row[...]
+    greet(
+        [at.sibling, at.over_x, at.over_y]
+        + [at.at_z(lax.rem(at.z + step, 4)) for step in (1, 2, 3)]
+    )
+    early.begin()
+    gathered.run()
+    placed = r.gain_all[...].reshape(32, 256)
+    pieces = []
+    for m in range(8):
+        for k in range(5):
+            piece = None
+            if k < 4:
+                piece = placed[4 * m + k : 4 * m + k + 1, :128]
+            if k > 0:
+                other = placed[4 * m + k - 1 : 4 * m + k, 128:]
+                piece = other if piece is None else piece + other
+            pieces.append(piece)
+    r.gains[...] = jnp.concatenate(pieces, axis=1)
+    gain = gain_parts(r)
+    residual = r.tokens[...].astype(jnp.float32)
+    r.normed[...] = (residual * rms_scale(residual) * gain[0]).astype(jnp.bfloat16)
+    early.first_half()
+    early.second_half()
+    late.begin()
+    early.settle()
+    normed = r.normed[...]
+    cos, sin = r.cos[...], r.sin[...]
+    mixed_rows = rows_of_all(w_all, 32, 16)
+    r.wk[...] = nn(pick(0), mixed_rows).astype(jnp.bfloat16)
+    r.wv[...] = nn(pick(8), mixed_rows).astype(jnp.bfloat16)
+    k_raw = nt(normed, r.wk[...])
+    r.k_raw[...] = k_raw
+    key = turn(k_raw * rms_scale(k_raw) * gain[2], cos, sin)
+    kv_all[s, :, :256] = key.astype(jnp.bfloat16)
+    kv_all[s, :, 256:] = nt(normed, r.wv[...]).astype(jnp.bfloat16)
+
+    def kv_copy(which, slot, device):
+        return remote(kv_all.at[slot], kv_all.at[slot], kv_out.at[which], kv_in.at[which], device)
+
+    peer_slot = lax.rem(s + 2, 4)
+    kv_copy(0, s, at.over_x).start()
+    kv_copy(1, s, at.sibling).start()
+    late.first_half()
+    kv_copy(0, peer_slot, at.over_x).wait_recv()
+    kv_copy(2, peer_slot, at.sibling).start()
+    for head in range(4):
+        q_raw = nt(normed, rows_of_head(w_all, head, 0, 32))
+        r.q_raw[:, columns_of(head)] = q_raw
+        query = turn(q_raw * rms_scale(q_raw) * gain[1], cos, sin)
+        r.query[:, columns_of(head)] = query.astype(jnp.bfloat16)
+    late.second_half()
+
+    def x_weight(k):
+        ref = (r.own_gate, r.own_up, r.own_down)[k]
+        return remote(ref, r.peer_w.at[k], x_out.at[k], x_in.at[k], at.over_x)
+
+    for k in range(3):
+        x_weight(k).start()
+    other = s + 1 - 2 * core
+    kv_copy(1, other, at.sibling).wait_recv()
+    kv_copy(2, lax.rem(other + 2, 4), at.sibling).wait_recv()
+    keys, values = kv_parts(r)
+    key_place = lax.broadcasted_iota(jnp.int32, (128, 512), 1)
+    query_place = lax.broadcasted_iota(jnp.int32, (128, 512), 0) + s * 128
+    allowed = (key_place >= r.doc[...]) & (key_place <= query_place)
+    for head in range(4):
+        raw = nt(r.query[:, columns_of(head)], keys) * score_step
+        scores = jnp.where(allowed, raw, hidden_score)
+        weights = jnp.exp(scores - jnp.max(scores, axis=1, keepdims=True))
+        prob = weights / jnp.sum(weights, axis=1, keepdims=True)
+        r.prob[head] = prob
+        mixed = nn(prob.astype(jnp.bfloat16), values).astype(jnp.bfloat16)
+        r.mixed[:, columns_of(head)] = mixed
+    late.settle()
+    attn = nn(r.mixed[...], rows_of_all(w_all, 48, 32))
+    r.attn[...] = attn
+    middle = r.tokens[...].astype(jnp.float32) + attn * rms_scale(attn) * gain[3]
+    r.middle[...] = middle
+    normed_ffn = (middle * rms_scale(middle) * gain[4]).astype(jnp.bfloat16)
+
+    def drain():
+        gathered.drain()
+        early.drain()
+        late.drain()
+        kv_copy(0, s, at.over_x).wait_send()
+        kv_copy(1, s, at.sibling).wait_send()
+        kv_copy(2, peer_slot, at.sibling).wait_send()
+
+    return normed_ffn, x_weight, drain
+
+
+def gain_parts(r):
+    return [r.gains[:, a:b] for a, b in zip(gain_edges[:-1], gain_edges[1:])]
+
+
+def kv_parts(r):
+    return r.kv_all[...].reshape(512, 512)[:, :256], r.kv_all[...].reshape(512, 512)[:, 256:]
+
+
+def ffn_phase(at, r, sems, normed_ffn, x_weight):
+    core = at.core
+    fwd_gather, fwd_sum = sems[:7], sems[7:13]
+    bwd_gather, bwd_sum = sems[13:20], sems[20:26]
+    x_out, x_in = sems[26:28]
+    sum_bufs = (r.to_sib, r.from_sib, r.chip_sum, r.from_y, r.to_z, r.from_z)
+    normed_all, grad_all = r.held.at[0], r.held.at[1]
+    gates = (r.own_gate, r.peer_w.at[0])
+    ups = (r.own_up, r.peer_w.at[1])
+    downs = (r.own_down, r.peer_w.at[2])
+    r.held[0, at.f, core] = normed_ffn
+
+    def rows_of(which, chip):
+        return jnp.concatenate([r.held[which, chip, core], r.held[which, chip, 1 - core]], axis=0)
+
+    def weights_here():
+        for k in range(3):
+            x_weight(k).wait()
+
+    def forward(chip):
+        rows = rows_of(0, chip)
+        total = None
+        for half in (0, 1):
+            gate = nt(rows, gates[half][...])
+            up = nt(rows, ups[half][...])
+            r.gate_keep[half, chip] = gate.astype(jnp.bfloat16)
+            r.up_keep[half, chip] = up.astype(jnp.bfloat16)
+            bend = jnp.tanh(gelu_c * (gate + 0.044715 * gate * gate * gate))
+            hidden = (0.5 * gate * (1.0 + bend) * up).astype(jnp.bfloat16)
+            part = nn(hidden, downs[half][...])
+            total = part if total is None else total + part
+        return total[:128], total[128:]
+
+    finish, drain = exchange_pass(
+        at, normed_all, fwd_gather, fwd_sum, sum_bufs, r.part_own, forward, 4, weights_here
+    )
+    ffn_raw = finish()
+    drain()
+    gain = gain_parts(r)[5]
+    scale = rms_scale(ffn_raw)
+    r.result[...] = (r.middle[...] + ffn_raw * scale * gain).astype(jnp.bfloat16)
+    ffn_grad, gain_grad = norm_back(ffn_raw, gain, r.cotangent[...].astype(jnp.float32))
+    r.gain_sum[:, gain_edges[5] : gain_edges[6]] = gain_grad
+    r.held[1, at.f, core] = ffn_grad.astype(jnp.bfloat16)
+    own_grads = (r.gate_grad, r.up_grad, r.down_grad)
+    grads = (own_grads, tuple(r.peer_sum.at[k] for k in range(3)))
+    for half in (0, 1):
+        for target in grads[half]:
+            target[...] = jnp.zeros(target.shape, jnp.float32)
+
+    def backward(chip):
+        rows = rows_of(1, chip)
+        ahead = rows_of(0, chip)
+        total = None
+        for half in (0, 1):
+            dhidden = nt(rows, downs[half][...])
+            gate = r.gate_keep[half, chip].astype(jnp.float32)
+            up = r.up_keep[half, chip].astype(jnp.float32)
+            square = gate * gate
+            bend = jnp.tanh(gelu_c * (gate + 0.044715 * square * gate))
+            unit = 0.5 * gate * (1.0 + bend)
+            slope = 0.5 * (1.0 + bend) + 0.5 * gate * (1.0 - bend * bend) * (
+                gelu_c * (1.0 + 3 * 0.044715 * square)
+            )
+            hidden = (unit * up).astype(jnp.bfloat16)
+            dgate = (dhidden * up * slope).astype(jnp.bfloat16)
+            dup = (dhidden * unit).astype(jnp.bfloat16)
+            part = nn(dgate, gates[half][...]) + nn(dup, ups[half][...])
+            total = part if total is None else total + part
+            gate_sum, up_sum, down_sum = grads[half]
+            gate_sum[...] += tn(dgate, ahead)
+            up_sum[...] += tn(dup, ahead)
+            down_sum[...] += tn(hidden, rows)
+        return total[:128], total[128:]
+
+    def x_copy(k):
+        return remote(r.peer_w.at[k], r.from_x.at[k], x_out.at[k], x_in.at[k], at.over_x)
+
+    def send_x():
+        for k in range(3):
+            r.peer_w[k] = r.peer_sum[k].astype(jnp.bfloat16)
+            x_copy(k).start()
+
+    finish, drain = exchange_pass(
+        at, grad_all, bwd_gather, bwd_sum, sum_bufs, r.part_own, backward, 0, None, send_x
+    )
+    normed_grad = finish()
+    drain()
+
+    def complete():
+        for k in range(3):
+            x_copy(k).wait()
+            own_grads[k][...] += r.from_x[k].astype(jnp.float32)
+
+    return normed_grad, complete
+
+
+def back_phase(at, r, sems, normed_grad, complete):
+    core, s = at.core, at.s
+    x = s // 2
+    gain = gain_parts(r)
+    cos, sin = r.cos[...], r.sin[...]
+    bufs = (r.sib_in, r.half_in, r.half_in, r.xf_in, r.yf_in, r.zw_in)
+    w_sems = sems[:12]
+    kv_out, kv_in = sems[12:14]
+    outer = WeightReturn(at, r.held, bufs, w_sems, 1, 48, 64, 80)
+    inner = WeightReturn(at, r.held, bufs, w_sems, 0, 0, 16, 48)
+    gain_total = GainSum(at, r.gain_sum, r.gain_out, r.gain_in, sems[14:16])
+
+    def put_gain(k, value):
+        r.gain_sum[:, gain_edges[k] : gain_edges[k + 1]] = value
+
+    def put_rows(head, low, count, rows):
+        split = rows.astype(jnp.bfloat16).reshape(4, 2, count, rows.shape[-1])
+        for c in range(4):
+            for k in (0, 1):
+                r.held[k, 2 * head + c // 2, c % 2, low : low + count] = split[c, k]
+
+    part, gain_grad = norm_back(r.middle[...], gain[4], normed_grad)
+    put_gain(4, gain_grad)
+    middle_grad = r.cotangent[...].astype(jnp.float32) + part
+    r.middle[...] = middle_grad
+    attn_grad, gain_grad = norm_back(r.attn[...], gain[3], middle_grad)
+    put_gain(3, gain_grad)
+    attn_grad = attn_grad.astype(jnp.bfloat16)
+    for head in range(4):
+        put_rows(head, 48, 32, tn(r.mixed[:, columns_of(head)], attn_grad))
+    outer.send_sib()
+    keys, values = kv_parts(r)
+    for head in range(4):
+        mixed_grad = nt(attn_grad, rows_of_head(r.w_all, head, 48, 32)).astype(jnp.bfloat16)
+        prob = r.prob[head]
+        prob_grad = nt(mixed_grad, values)
+        delta = jnp.sum(prob * prob_grad, axis=1, keepdims=True)
+        score_grad = (prob * (prob_grad - delta)).astype(jnp.bfloat16)
+        key_part = tn(score_grad, r.query[:, columns_of(head)]) * score_step
+        value_part = tn(prob.astype(jnp.bfloat16), mixed_grad)
+        if head == 0:
+            r.kv_sum[:, :256] = key_part
+            r.kv_sum[:, 256:] = value_part
+        else:
+            r.kv_sum[:, :256] += key_part
+            r.kv_sum[:, 256:] += value_part
+        r.query_grad[:, columns_of(head)] = nn(score_grad, keys) * score_step
+    r.kv_part[...] = r.kv_sum[...].astype(jnp.bfloat16).reshape(2, 2, 128, 512)
+    kv_sib = remote(
+        r.kv_part.at[:, 1 - core], r.kv_sib.at[...], kv_out.at[0], kv_in.at[0], at.sibling
+    )
+    kv_sib.start()
+    outer.merge()
+    kv_sib.wait_recv()
+    r.kv_chip[...] = (
+        r.kv_part[1 - x, core].astype(jnp.float32) + r.kv_sib[1 - x].astype(jnp.float32)
+    ).astype(jnp.bfloat16)
+    kv_x = remote(r.kv_chip, r.kv_far, kv_out.at[1], kv_in.at[1], at.over_x)
+    kv_x.start()
+    normed = r.normed[...]
+    query_gain = None
+    for head in range(4):
+        turned = turn_back(r.query_grad[:, columns_of(head)], cos, sin)
+        q_raw_grad, gain_grad = norm_back(r.q_raw[:, columns_of(head)], gain[1], turned)
+        query_gain = gain_grad if query_gain is None else query_gain + gain_grad
+        q_raw_grad = q_raw_grad.astype(jnp.bfloat16)
+        r.query[:, columns_of(head)] = q_raw_grad
+        put_rows(head, 0, 32, tn(q_raw_grad, normed))
+    put_gain(1, query_gain)
+    outer.pair_up()
+    kv_x.wait_recv()
+    kv_grad = (
+        r.kv_part[x, core].astype(jnp.float32)
+        + r.kv_sib[x].astype(jnp.float32)
+        + r.kv_far[...].astype(jnp.float32)
+    )
+    k_raw_grad, gain_grad = norm_back(r.k_raw[...], gain[2], turn_back(kv_grad[:, :256], cos, sin))
+    put_gain(2, gain_grad)
+    k_raw_grad = k_raw_grad.astype(jnp.bfloat16)
+    v_raw_grad = kv_grad[:, 256:].astype(jnp.bfloat16)
+    woven = (nn(k_raw_grad, pick(0)) + nn(v_raw_grad, pick(8))).astype(jnp.bfloat16)
+    for head in range(4):
+        put_rows(head, 32, 16, tn(woven[:, 128 * head : 128 * head + 128], normed))
+    inner.send_sib()
+    normed_grad = nn(k_raw_grad, r.wk[...]) + nn(v_raw_grad, r.wv[...])
+    for head in range(4):
+        normed_grad += nn(r.query[:, columns_of(head)], rows_of_head(r.w_all, head, 0, 32))
+    part, gain_grad = norm_back(r.tokens[...].astype(jnp.float32), gain[0], normed_grad)
+    put_gain(0, gain_grad)
+    gain_total.send(0)
+    r.token_grad[...] = r.middle[...] + part
+    inner.merge()
+    gain_total.take(0)
+    gain_total.send(1)
+    outer.collect()
+    inner.pair_up()
+    gain_total.take(1)
+    gain_total.send(2)
+    inner.collect()
+    gain_total.take(2)
+    gain_total.send(3)
+    r.o_grad[...] = outer.total()
+    complete()
+    total = inner.total()
+    r.q_grad[...] = total[:32]
+    r.k_grad[...] = total[32:40]
+    r.v_grad[...] = total[40:48]
+    gain_total.take(3)
+    outer.drain()
+    inner.drain()
+    gain_total.drain()
+    kv_sib.wait_send()
+    kv_x.wait_send()
+
+
+def layer_call(values):
+    b16, f32 = jnp.bfloat16, jnp.float32
+    rows, width = values["tokens"].shape
+    units = values["own_gate"].shape[0]
+    outs = {
+        "result": ((rows, width), b16),
+        "token_grad": ((rows, width), f32),
+        "gain_sum": ((1, 5120), f32),
+        "q_grad": ((32, width), f32),
+        "k_grad": ((8, width), f32),
+        "v_grad": ((8, width), f32),
+        "o_grad": ((32, width), f32),
+        "gate_grad": ((units, width), f32),
+        "up_grad": ((units, width), f32),
+        "down_grad": ((units, width), f32),
+    }
+    scratch = {
+        "w_all": ((16, 2, 80, width), b16),
+        "gain_all": ((32, 1, 256), f32),
+        "gains": ((1, 5120), f32),
+        "wk": ((256, width), b16),
+        "wv": ((256, width), b16),
+        "normed": ((rows, width), b16),
+        "k_raw": ((rows, 256), f32),
+        "q_raw": ((rows, 1024), f32),
+        "query": ((rows, 1024), b16),
+        "query_grad": ((rows, 1024), f32),
+        "kv_all": ((4, rows, 512), b16),
+        "prob": ((4, rows, 512), f32),
+        "mixed": ((rows, 1024), b16),
+        "attn": ((rows, width), f32),
+        "middle": ((rows, width), f32),
+        "peer_w": ((3, units, width), b16),
+        "held": ((2, 8, 2, rows, width), b16),
+        "gate_keep": ((2, 8, 2 * rows, units), b16),
+        "up_keep": ((2, 8, 2 * rows, units), b16),
+        "peer_sum": ((3, units, width), f32),
+        "part_own": ((rows, width), f32),
+        "to_sib": ((8, rows, width), b16),
+        "from_sib": ((8, rows, width), b16),
+        "chip_sum": ((8, rows, width), b16),
+        "from_y": ((4, rows, width), b16),
+        "to_z": ((4, rows, width), b16),
+        "from_z": ((2, 4, rows, width), b16),
+        "from_x": ((3, units, width), b16),
+        "sib_in": ((8, 2, 80, width), b16),
+        "half_in": ((4, 80, width), b16),
+        "xf_in": ((4, 80, width), b16),
+        "yf_in": ((4, 80, width), b16),
+        "zw_in": ((4, 80, width), b16),
+        "kv_sum": ((4 * rows, 512), f32),
+        "kv_part": ((2, 2, rows, 512), b16),
+        "kv_sib": ((2, rows, 512), b16),
+        "kv_chip": ((rows, 512), b16),
+        "kv_far": ((rows, 512), b16),
+        "gain_out": ((4, 1, 5120), f32),
+        "gain_in": ((7, 1, 5120), f32),
+    }
+    gather_sems = [DMA((2,)), DMA((4,)), DMA((4,)), DMA((4,)), DMA((4,)), DMA((8,)), DMA((8,))]
+    sum_sems = [DMA((8,)), DMA((8,)), DMA((4,)), DMA((4,)), DMA((4,)), DMA((2, 4))]
+    front_sems = gain_sems() + gather_weight_sems() + [DMA((3,))] * 4
+    ffn_sems = (gather_sems + sum_sems) * 2 + [DMA((3,)), DMA((3,))]
+    back_sems = [DMA((2, 4))] * 12 + [DMA((2,)), DMA((2,)), DMA((6,)), DMA((7,))]
+    sems = front_sems + ffn_sems + back_sems
+    names = tuple(values) + tuple(outs) + tuple(scratch)
+
+    def kernel(*refs):
+        at = Place()
+        r = Refs(names, refs)
+        held_sems = refs[len(names) :]
+        first, second = len(front_sems), len(front_sems) + len(ffn_sems)
+        normed_ffn, x_weight, drain = front_phase(at, r, held_sems[:first])
+        normed_grad, complete = ffn_phase(at, r, held_sems[first:second], normed_ffn, x_weight)
+        back_phase(at, r, held_sems[second:], normed_grad, complete)
+        drain()
+
+    vmem = pl.BlockSpec(memory_space=pltpu.VMEM)
+    out = pl.pallas_call(
+        kernel,
+        out_shape=tuple(jax.ShapeDtypeStruct(*spec) for spec in outs.values()),
+        in_specs=[vmem] * len(values),
+        out_specs=tuple([vmem] * len(outs)),
+        scratch_shapes=[pltpu.VMEM(*spec) for spec in scratch.values()] + sems,
+        compiler_params=pltpu.CompilerParams(
+            collective_id=1, has_side_effects=True, vmem_limit_bytes=63 << 20
+        ),
+        name="layer",
+    )(*values.values())
+    return dict(zip(outs, out))
+
+
+def one_kernel(
+    tokens, doc_start, gains, w_query, w_key, w_value, w_out, w_gate, w_up, w_down, cotangent
+):
+    rows = tokens.shape[0]
+    device = lax.axis_index("fsdp") * lax.axis_size("seq") + lax.axis_index("seq")
+    share = gains.shape[0]
+    gain_row = lax.dynamic_update_slice(
+        jnp.zeros((1, 256), jnp.float32),
+        gains[None].astype(jnp.float32),
+        (0, lax.rem(device, 4) * 32),
+    )
+    places = lax.axis_index("seq") * rows + jnp.arange(rows, dtype=jnp.int32) - doc_start
+    cos, sin = rope_tables(places, 256)
+    out = layer_call(
+        {
+            "tokens": tokens,
+            "doc": doc_start[:, None],
+            "gain_row": gain_row,
+            "own_q": w_query.T,
+            "own_k": w_key.T,
+            "own_v": w_value.T,
+            "own_o": w_out,
+            "own_gate": w_gate.T,
+            "own_up": w_up.T,
+            "own_down": w_down,
+            "cos": cos[:, 0],
+            "sin": sin[:, 0],
+            "cotangent": cotangent,
+        }
+    )
+    return (
+        out["result"],
+        out["token_grad"],
+        lax.dynamic_slice(out["gain_sum"][0], (device * share,), (share,)),
+        out["q_grad"].T,
+        out["k_grad"].T,
+        out["v_grad"].T,
+        out["o_grad"],
+        out["gate_grad"].T,
+        out["up_grad"].T,
+        out["down_grad"],
+    )
+
+
 def solution(mesh):
     in_specs = (
         P(("fsdp", "seq"), None),
@@ -284,4 +1492,5 @@
         P(None, ("fsdp", "seq")),
         P(("fsdp", "seq"), None),
     )
-    return jax.shard_map(local, mesh=mesh, in_specs=in_specs, out_specs=out_specs, check_vma=False)
+    body = one_kernel if dict(mesh.shape) == {"fsdp": 8, "seq": 4} else local
+    return jax.shard_map(body, mesh=mesh, in_specs=in_specs, out_specs=out_specs, check_vma=False)

time: 1910 us -> 262 us (0.14)
  waiting for transfers between devices: 1510 us -> 0 us
  Pallas kernels: 0 us -> 247 us
  blocking collectives: 195 us -> 0 us
  matrix products: 128 us -> 0 us
    unnamed x17 -> x0, waiting for transfers between devices: 982 us -> none
    all_gather x5 -> x0, waiting for transfers between devices: 261 us -> none  [the longest x1 100 us: local(): lax.all_gather(w_up, ('fsdp', 'seq'), axis=1, tiled=True)]
    reduce_scatter x4 -> x0, waiting for transfers between devices: 256 us -> none  [the longest x1 112 us: local(): lax.psum_scatter(query_w_grad_t, ('fsdp', 'seq'), scatter_dimension=0, ti...]
    pallas_call x0 -> x1, Pallas kernels: none -> 247 us  [layer_call(): pl.pallas_call(kernel, out_shape=tuple((jax.ShapeDtypeStruct(*spec) for s...]
    dot_general x27 -> x0, matrix products: 128 us -> none  [the longest x9 53.4 us: inner_rows(): lax.dot_general(former, latter, (((0,), (0,)), ((), ())), preferred_eleme...]
    all_gather x5 -> x0, blocking collectives: 103 us -> none  [the longest x1 42.3 us: local(): lax.all_gather(w_key, ('fsdp', 'seq'), axis=1, tiled=True)]
    unnamed x2 -> x0, blocking collectives: 81.1 us -> none
  transfers between devices with their start and end apart: 16 -> 0, of which waited for: 13 -> 0; matrix products, arithmetic and copies ran while one was open for 6% -> 0% of each run, Pallas kernels for 0% -> 0%
where the time goes in v3:
time: 262 us
  Pallas kernels  247 us (94%)
  local copies, waits for them, and re-layouts  13.1 us (5%)
    pallas_call x1, Pallas kernels, layer_call(): pl.pallas_call(kernel, out_shape=tuple((jax.ShapeDtypeStruct(*spec) for s...  247 us
    unnamed x31, local copies, waits for them, and re-layouts  10.9 us

profile of v3, /device:TPU:0, one launch (start us, length us, event | category | flops | bytes accessed | tf_op | source)
XLA Modules:
  0.0 261.5 jit_solution(11103912102973931897)
XLA Ops:
  0.7 0.0 copy-start.9
  0.7 0.6 copy-done.9
  1.3 0.6 copy-done.10
  2.0 0.1 dynamic_update_slice.3.refs_2_
  2.1 0.0 copy-start.8
  2.1 0.7 copy.21.refs_1_
  2.8 1.0 multiply_sine_fusion
  3.8 246.7 %layer.1 = (bf16[128,1152]{1,0:T(8,128)(2,1)}, f32[128,1152]{1,0:T(8,128)}, f32[1,5120]{1,0:T(1,128)}, f32[32,1152]{1,0:T(8,128)}, f32[8,1152]{1,0:T(8,128)}, /*...) custom-call(bf16[128,1152]{1,0:T(8,128)(2,1)} %refs_0_.1, ...), custom_call_target="tpu_custom_call" | custom-call | tf_op jit(solution)/shard_map/layer/pallas_call | solution.py:1411
  250.5 1.3 constant_dynamic-slice_fusion
  251.9 1.7 copy.32
  253.6 0.8 copy.33
  254.4 0.2 copy-done.5
  254.6 0.7 copy.34
  255.3 0.1 copy-done.7
  255.4 0.6 copy.35
  256.0 0.2 copy-done.6
  256.1 0.6 copy.36
  256.8 0.0 copy-done.4
  256.8 0.7 copy.37
  257.4 0.9 copy.38
  258.4 0.6 copy-done.1
  259.0 0.9 copy.39
  259.9 0.6 copy-done
  260.6 0.9 copy.40
  (16 shorter events, 0.0 us)
Async XLA Ops:
  0.7 0.7 copy-start.9
  1.3 0.7 copy-start.10
  2.1 0.8 copy-start.8
  250.5 3.1 %copy-start.3 = (f32[128,1152]{1,0:T(8,128)S(1)}, f32[128,1152]{1,0:T(8,128)}, u32[]{:S(2)}) copy-start(f32[128,1152]{1,0:T(8,128)} %get-tuple-element.43) | copy-start | bytes 1769476
  253.6 1.0 copy-start.5
  253.6 3.9 %copy-start.2 = (f32[216,1152]{1,0:T(8,128)S(1)}, f32[216,1152]{1,0:T(8,128)}, u32[]{:S(2)}) copy-start(f32[216,1152]{1,0:T(8,128)} %get-tuple-element.27) | copy-start | bytes 2985988
  254.6 0.8 copy-start.7
  254.6 2.2 copy-start.4
  255.4 0.8 copy-start.6
  257.4 1.6 copy-start.1
  259.0 1.6 copy-start

commit v4 on v3

--- a/solution.py
+++ b/solution.py
@@ -598,15 +598,21 @@
         span = self.held.at[pl.ds(src * 8, 8)]
         return remote(span, span, self.z_out.at[j], self.z_in.at[src], device)
 
-    def run(self):
+    def send(self, k):
         at = self.at
-        for k in range(3):
+        if k < 3:
             self.stage(k).start()
+        else:
+            for j in (1, 2, 3):
+                self.last(at.z, j, at.at_z(at.source(j))).start()
+
+    def take(self, k):
+        at = self.at
+        if k < 3:
             self.stage(k).wait_recv()
-        for j in (1, 2, 3):
-            self.last(at.z, j, at.at_z(at.source(j))).start()
-        for j in (1, 2, 3):
-            self.last(at.source(j), j, at.at_z(at.source(j))).wait_recv()
+        else:
+            for j in (1, 2, 3):
+                self.last(at.source(j), j, at.at_z(at.source(j))).wait_recv()
 
     def drain(self):
         at = self.at
@@ -617,77 +623,73 @@
 
 
 class WeightGather:
-    def __init__(self, at, w_all, sems, part, low, middle, high):
+    def __init__(self, at, w_all, sems, part, low, high):
         self.at, self.w_all, self.part = at, w_all, part
         (
+            self.x_out,
+            self.x_in,
+            self.first_out,
+            self.first_in,
             self.z_own,
             self.z_next,
             self.z_in,
-            self.yf_out,
-            self.yf_in,
-            self.xf_out,
-            self.xf_in,
-            self.yh_out,
-            self.yh_in,
-            self.xh_out,
-            self.xh_in,
+            self.y_out,
+            self.y_in,
             self.s_out,
             self.s_in,
         ) = sems
-        self.low, self.middle, self.high = low, middle, high
+        self.rows = pl.ds(low, high - low)
         self.x = at.s // 2
 
-    def block(self, z, y, x, low, high):
-        chip = (z * 2 + y) * 2 + x
-        return self.w_all.at[chip, self.at.core, pl.ds(low, high - low)]
-
-    def whole(self, z, outgoing, incoming, device):
-        span = self.block(z, self.at.y, self.x, self.low, self.high)
+    def one(self, y, x, outgoing, incoming, device):
+        span = self.w_all.at[(self.at.z * 2 + y) * 2 + x, self.at.core, self.rows]
         return remote(span, span, outgoing, incoming, device)
 
+    def pair(self, z, y, outgoing, incoming, device):
+        span = self.w_all.at[pl.ds((z * 2 + y) * 2, 2), self.at.core, self.rows]
+        return remote(span, span, outgoing, incoming, device)
+
+    def x_copy(self, x):
+        p, at = self.part, self.at
+        return self.one(at.y, x, self.x_out.at[p], self.x_in.at[p], at.over_x)
+
+    def y_first(self, y, x):
+        p, at = self.part, self.at
+        return self.one(y, x, self.first_out.at[p, x], self.first_in.at[p, x], at.over_y)
+
     def own(self, step, slot):
-        at, p = self.at, self.part
-        return self.whole(at.z, self.z_own.at[p, slot], self.z_in.at[p, at.z], at.at_z(at.z + step))
+        p, at = self.part, self.at
+        return self.pair(
+            at.z, at.y, self.z_own.at[p, slot], self.z_in.at[p, at.z], at.at_z(at.z + step)
+        )
 
     def passed(self, src, device):
         p = self.part
-        return self.whole(src, self.z_next.at[p, src], self.z_in.at[p, src], device)
-
-    def y_full(self, src):
+        return self.pair(src, self.at.y, self.z_next.at[p, src], self.z_in.at[p, src], device)
+
+    def y_pair(self, src, y):
         p = self.part
-        return self.whole(src, self.yf_out.at[p, src], self.yf_in.at[p, src], self.at.over_y)
-
-    def x_full(self, src):
-        p = self.part
-        return self.whole(src, self.xf_out.at[p, src], self.xf_in.at[p, src], self.at.over_x)
-
-    def x_half(self, src):
-        span = self.block(src, 1 - self.at.y, self.x, self.low, self.middle)
-        p = self.part
-        return remote(span, span, self.xh_out.at[p, src], self.xh_in.at[p, src], self.at.over_x)
-
-    def y_half(self, src):
-        span = self.block(src, self.at.y, 1 - self.x, self.middle, self.high)
-        p = self.part
-        return remote(span, span, self.yh_out.at[p, src], self.yh_in.at[p, src], self.at.over_y)
+        return self.pair(src, y, self.y_out.at[p, src], self.y_in.at[p, src], self.at.over_y)
 
     def sib(self, src):
-        span = self.w_all.at[
-            pl.ds(src * 4, 4), self.at.core, pl.ds(self.low, self.high - self.low)
-        ]
+        span = self.w_all.at[pl.ds(src * 4, 4), self.at.core, self.rows]
         p = self.part
         return remote(span, span, self.s_out.at[p, src], self.s_in.at[p, src], self.at.sibling)
 
     def begin(self):
+        self.x_copy(self.x).start()
+
+    def spread(self):
         at = self.at
+        self.y_first(at.y, self.x).start()
+        self.x_copy(1 - self.x).wait_recv()
         self.own(at.toward, 0).start()
 
         @pl.when(at.inner)
         def _():
             self.own(-at.toward, 1).start()
 
-        self.y_full(at.z).start()
-        self.x_full(at.z).start()
+        self.y_first(at.y, 1 - self.x).start()
 
     def take(self, j):
         at = self.at
@@ -698,31 +700,28 @@
         def _():
             self.passed(src, at.at_z(at.z + (at.toward if j == 1 else -at.toward))).start()
 
-        self.y_full(src).start()
-        self.x_full(src).start()
-
-    def cross(self, j):
-        src = self.at.source(j)
-        self.y_full(src).wait_recv()
-        self.x_half(src).start()
-        self.x_full(src).wait_recv()
-        self.y_half(src).start()
+        self.y_pair(src, at.y).start()
 
     def close(self, j):
         src = self.at.source(j)
-        self.x_half(src).wait_recv()
-        self.y_half(src).wait_recv()
+        if j == 0:
+            for x in (0, 1):
+                self.y_first(1 - self.at.y, x).wait_recv()
+        else:
+            self.y_pair(src, 1 - self.at.y).wait_recv()
         self.sib(src).start()
 
-    def first_half(self):
+    def walk(self, between=()):
         at = self.at
+        extra = list(between) + [lambda: None] * 3
         self.take(1)
 
         @pl.when(at.inner)
         def _():
             self.take(2)
 
-        self.cross(0)
+        extra[0]()
+        self.close(0)
 
         @pl.when(at.inner)
         def _():
@@ -732,17 +731,14 @@
         def _():
             self.take(2)
 
-        self.cross(1)
-        self.close(0)
-
-    def second_half(self):
-        @pl.when(self.at.outer)
+        extra[1]()
+        self.close(1)
+
+        @pl.when(at.outer)
         def _():
             self.take(3)
 
-        self.cross(2)
-        self.close(1)
-        self.cross(3)
+        extra[2]()
         self.close(2)
         self.close(3)
 
@@ -752,6 +748,9 @@
 
     def drain(self):
         at = self.at
+        self.x_copy(self.x).wait_send()
+        for x in (0, 1):
+            self.y_first(at.y, x).wait_send()
         self.own(at.toward, 0).wait_send()
 
         @pl.when(at.inner)
@@ -762,12 +761,13 @@
 
         for j in range(4):
             src = at.source(j)
-            for copy in (self.y_full, self.x_full, self.x_half, self.y_half, self.sib):
-                copy(src).wait_send()
+            if j > 0:
+                self.y_pair(src, at.y).wait_send()
+            self.sib(src).wait_send()
 
 
 def gather_weight_sems():
-    return [DMA((2, 2))] + [DMA((2, 4))] * 12
+    return [DMA((2,)), DMA((2,))] + [DMA((2, 2))] * 3 + [DMA((2, 4))] * 6
 
 
 def gain_sems():
@@ -1008,11 +1008,11 @@
 def front_phase(at, r, sems):
     core, s = at.core, at.s
     gathered = GainGather(at, r.gain_all, sems[:4])
-    w_sems = sems[4:17]
-    kv_out, kv_in, x_out, x_in = sems[17:21]
+    w_sems = sems[4:15]
+    kv_out, kv_in, x_out, x_in = sems[15:19]
     w_all, kv_all = r.w_all, r.kv_all
-    early = WeightGather(at, w_all, w_sems, 0, 0, 16, 48)
-    late = WeightGather(at, w_all, w_sems, 1, 48, 64, 80)
+    early = WeightGather(at, w_all, w_sems, 0, 0, 48)
+    late = WeightGather(at, w_all, w_sems, 1, 48, 80)
     chip = at.f * 2 + s // 2
     w_all[chip, core, 0:32] = r.own_q[...]
     w_all[chip, core, 32:48] = jnp.concatenate(
@@ -1024,8 +1024,27 @@
         [at.sibling, at.over_x, at.over_y]
         + [at.at_z(lax.rem(at.z + step, 4)) for step in (1, 2, 3)]
     )
+    def x_weight(k):
+        ref = (r.own_gate, r.own_up, r.own_down)[k]
+        return remote(ref, r.peer_w.at[k], x_out.at[k], x_in.at[k], at.over_x)
+
+    def gain_step(k):
+        def step():
+            gathered.take(k)
+            if k < 3:
+                gathered.send(k + 1)
+
+        return step
+
+    gathered.send(0)
     early.begin()
-    gathered.run()
+    late.begin()
+    gain_step(0)()
+    early.spread()
+    x_weight(0).start()
+    x_weight(1).start()
+    gain_step(1)()
+    early.walk((gain_step(2), gain_step(3), late.spread))
     placed = r.gain_all[...].reshape(32, 256)
     pieces = []
     for m in range(8):
@@ -1041,9 +1060,6 @@
     gain = gain_parts(r)
     residual = r.tokens[...].astype(jnp.float32)
     r.normed[...] = (residual * rms_scale(residual) * gain[0]).astype(jnp.bfloat16)
-    early.first_half()
-    early.second_half()
-    late.begin()
     early.settle()
     normed = r.normed[...]
     cos, sin = r.cos[...], r.sin[...]
@@ -1062,22 +1078,21 @@
     peer_slot = lax.rem(s + 2, 4)
     kv_copy(0, s, at.over_x).start()
     kv_copy(1, s, at.sibling).start()
-    late.first_half()
-    kv_copy(0, peer_slot, at.over_x).wait_recv()
-    kv_copy(2, peer_slot, at.sibling).start()
-    for head in range(4):
+
+    def one_query(head):
         q_raw = nt(normed, rows_of_head(w_all, head, 0, 32))
         r.q_raw[:, columns_of(head)] = q_raw
         query = turn(q_raw * rms_scale(q_raw) * gain[1], cos, sin)
         r.query[:, columns_of(head)] = query.astype(jnp.bfloat16)
-    late.second_half()
-
-    def x_weight(k):
-        ref = (r.own_gate, r.own_up, r.own_down)[k]
-        return remote(ref, r.peer_w.at[k], x_out.at[k], x_in.at[k], at.over_x)
-
-    for k in range(3):
-        x_weight(k).start()
+
+    def pass_kv():
+        one_query(0)
+        kv_copy(0, peer_slot, at.over_x).wait_recv()
+        kv_copy(2, peer_slot, at.sibling).start()
+        x_weight(2).start()
+        one_query(1)
+
+    late.walk((pass_kv, lambda: one_query(2), lambda: one_query(3)))
     other = s + 1 - 2 * core
     kv_copy(1, other, at.sibling).wait_recv()
     kv_copy(2, lax.rem(other + 2, 4), at.sibling).wait_recv()
@@ -1153,7 +1168,7 @@
         return total[:128], total[128:]
 
     finish, drain = exchange_pass(
-        at, normed_all, fwd_gather, fwd_sum, sum_bufs, r.part_own, forward, 4, weights_here
+        at, normed_all, fwd_gather, fwd_sum, sum_bufs, r.part_own, forward, 0, weights_here
     )
     ffn_raw = finish()
     drain()
@@ -1324,6 +1339,11 @@
     r.k_grad[...] = total[32:40]
     r.v_grad[...] = total[40:48]
     gain_total.take(3)
+    device = at.f * 4 + s
+    first = pl.multiple_of(device * 160 // 128 * 128, 128)
+    r.gain_grad[...] = pltpu.roll(
+        r.gain_sum[:, pl.ds(first, 256)], 256 - lax.rem(device, 4) * 32, 1
+    )
     outer.drain()
     inner.drain()
     gain_total.drain()
@@ -1338,7 +1358,7 @@
     outs = {
         "result": ((rows, width), b16),
         "token_grad": ((rows, width), f32),
-        "gain_sum": ((1, 5120), f32),
+        "gain_grad": ((1, 256), f32),
         "q_grad": ((32, width), f32),
         "k_grad": ((8, width), f32),
         "v_grad": ((8, width), f32),
@@ -1348,6 +1368,7 @@
         "down_grad": ((units, width), f32),
     }
     scratch = {
+        "gain_sum": ((1, 5120), f32),
         "w_all": ((16, 2, 80, width), b16),
         "gain_all": ((32, 1, 256), f32),
         "gains": ((1, 5120), f32),
@@ -1422,6 +1443,31 @@
     return dict(zip(outs, out))
 
 
+def settle_kernel(count, *refs):
+    ins, outs, held, sems = refs[:count], refs[count : 2 * count], refs[2 * count : -1], refs[-1]
+    loads = [pltpu.make_async_copy(ins[k], held[k], sems.at[0, k]) for k in range(count)]
+    stores = [pltpu.make_async_copy(held[k], outs[k], sems.at[1, k]) for k in range(count)]
+    for copy in loads:
+        copy.start()
+    for load, store in zip(loads, stores):
+        load.wait()
+        store.start()
+    for copy in stores:
+        copy.wait()
+
+
+def settle(arrays):
+    anywhere = pl.BlockSpec(memory_space=pl.ANY)
+    return pl.pallas_call(
+        partial(settle_kernel, len(arrays)),
+        out_shape=tuple(jax.ShapeDtypeStruct(a.shape, a.dtype) for a in arrays),
+        in_specs=[anywhere] * len(arrays),
+        out_specs=tuple([anywhere] * len(arrays)),
+        scratch_shapes=[pltpu.VMEM(a.shape, a.dtype) for a in arrays] + [DMA((2, len(arrays)))],
+        name="settle",
+    )(*arrays)
+
+
 def one_kernel(
     tokens, doc_start, gains, w_query, w_key, w_value, w_out, w_gate, w_up, w_down, cotangent
 ):
@@ -1452,10 +1498,13 @@
             "cotangent": cotangent,
         }
     )
+    names = ("result", "token_grad", "gain_grad", "q_grad", "k_grad", "v_grad", "o_grad")
+    names += ("gate_grad", "up_grad", "down_grad")
+    out = dict(zip(names, settle([out[name] for name in names])))
     return (
         out["result"],
         out["token_grad"],
-        lax.dynamic_slice(out["gain_sum"][0], (device * share,), (share,)),
+        out["gain_grad"][0, :share],
         out["q_grad"].T,
         out["k_grad"].T,
         out["v_grad"].T,

time: 262 us -> 241 us (0.920)
  Pallas kernels: 247 us -> 236 us
  local copies, waits for them, and re-layouts: 13.1 us -> 2.12 us
    pallas_call x1, Pallas kernels: 247 us -> 232 us  [layer_call(): pl.pallas_call(kernel, out_shape=tuple((jax.ShapeDtypeStruct(*spec) for s...]
    unnamed x31 -> x6, local copies, waits for them, and re-layouts: 10.9 us -> 1.3 us
    pallas_call x0 -> x1, Pallas kernels: none -> 3.99 us  [settle(): pl.pallas_call(partial(settle_kernel, len(arrays)), out_shape=tuple((jax....]
where the time goes in v4:
time: 241 us; the launch traced here: 240 us
  Pallas kernels  236 us (98%)
    pallas_call x1, Pallas kernels, layer_call(): pl.pallas_call(kernel, out_shape=tuple((jax.ShapeDtypeStruct(*spec) for s...  232 us

profile of v4, /device:TPU:0, one launch (start us, length us, event | category | flops | bytes accessed | tf_op | source)
XLA Modules:
  0.0 240.4 jit_solution(11769334512154627651)
XLA Ops:
  0.7 0.0 copy-start.1
  0.7 0.6 copy-done.1
  1.3 0.0 copy-start.2
  1.3 0.6 copy-done.2
  2.0 0.1 dynamic_update_slice.3.refs_2_
  2.1 0.0 copy-start
  2.1 0.7 copy.21.refs_1_
  2.8 0.0 copy-done
  2.8 1.0 multiply_sine_fusion
  3.8 232.4 %layer.1 = (bf16[128,1152]{1,0:T(8,128)(2,1)}, f32[128,1152]{1,0:T(8,128)}, f32[1,256]{1,0:T(1,128)}, f32[32,1152]{1,0:T(8,128)}, f32[8,1152]{1,0:T(8,128)}, /*i...) custom-call(bf16[128,1152]{1,0:T(8,128)(2,1)} %refs_0_.1, ...), custom_call_target="tpu_custom_call" | custom-call | tf_op jit(solution)/shard_map/layer/pallas_call | solution.py:1432
  236.2 4.0 %settle.1 = (bf16[128,1152]{1,0:T(8,128)(2,1)}, f32[128,1152]{1,0:T(8,128)}, f32[1,256]{1,0:T(1,128)}, f32[32,1152]{1,0:T(8,128)}, f32[8,1152]{1,0:T(8,128)}, /*...) custom-call(bf16[128,1152]{1,0:T(8,128)(2,1)} %get-tuple-element.30., ...), custom_call_target="tpu_custom_call" | custom-call | tf_op jit(solution)/shard_map/settle/pallas_call | solution.py:1461
  (4 shorter events, 0.0 us)
Async XLA Ops:
  0.7 0.7 copy-start.1
  1.3 0.7 copy-start.2
  2.1 0.8 copy-start

commit v5 on v4

--- a/solution.py
+++ b/solution.py
@@ -333,7 +333,7 @@
     pl.semaphore_wait(entry, len(partners))
 
 
-def exchange_pass(at, held, gather_sems, sum_sems, sum_bufs, part_own, compute, lag=0, ready=None, then=None):
+def exchange_pass(at, held, gather_sems, sum_sems, sum_bufs, part_own, compute, lag=0, ready=None, then=()):
     z_own, z_next, z_in, y_out, y_in, c_out, c_in = gather_sems
     t_out, t_in, v_out, v_in, w_out, w_in = sum_sems
     to_sib, from_sib, chip_sum, from_y, to_z, from_z = sum_bufs
@@ -392,8 +392,21 @@
     def sib_sum(i):
         return remote(to_sib.at[i], from_sib.at[i], t_out.at[i], t_in.at[i], at.sibling)
 
-    def y_sum(i):
-        return remote(chip_sum.at[i], from_y.at[i // 2], v_out.at[i // 2], v_in.at[i // 2], at.over_y)
+    rows = part_own.shape[0] // 4
+    pieces = [pl.ds(k * rows, rows) for k in range(4)]
+
+    def y_sum(i, k):
+        return remote(
+            chip_sum.at[i, pieces[k]],
+            from_y.at[i // 2, pieces[k]],
+            v_out.at[i // 2, k],
+            v_in.at[i // 2, k],
+            at.over_y,
+        )
+
+    def send_y(i):
+        for k in range(4):
+            y_sum(i, k).start()
 
     def finish_chip(i):
         sib_sum(i).wait_recv()
@@ -439,6 +452,10 @@
         def _():
             arrivals(i)
 
+        @pl.when(i == 7 + lag)
+        def _():
+            send_y(5)
+
         if ready is not None:
 
             @pl.when(i == lag)
@@ -453,61 +470,61 @@
 
     lax.fori_loop(0, 8 + lag, step, 0)
     finish_chip(7)
-    for j in (3, 2, 1, 0):
-        y_sum(2 * j + 1).start()
-    if then is not None:
-        then()
-
-    def z_sum(target, direction):
+    for j in (3, 1, 0):
+        send_y(2 * j + 1)
+    later = list(then) + [lambda: None] * 4
+    later[0]()
+
+    def z_sum(target, direction, k, device=None):
         slot = (direction + 1) // 2
         return remote(
-            to_z.at[target],
-            from_z.at[slot, target],
-            w_out.at[target],
-            w_in.at[slot, target],
-            at.at_z(at.z + direction),
+            to_z.at[target, pieces[k]],
+            from_z.at[slot, target, pieces[k]],
+            w_out.at[target, k],
+            w_in.at[slot, target, k],
+            at.at_z(at.z + direction) if device is None else device,
         )
 
-    def z_arrival(target, direction):
-        slot = (direction + 1) // 2
-        return remote(
-            to_z.at[target],
-            from_z.at[slot, target],
-            w_out.at[target],
-            w_in.at[slot, target],
-            at.at_z(lax.rem(at.z - direction + 4, 4)),
-        )
+    def z_arrival(target, direction, k):
+        return z_sum(target, direction, k, at.at_z(lax.rem(at.z - direction + 4, 4)))
 
     def direction_of(j):
         return at.step_first if j == 1 else at.toward
 
-    for j in (3, 2, 1):
+    for place, j in enumerate((2, 3, 1)):
         target, direction = at.source(j), direction_of(j)
-        y_sum(2 * j + 1).wait_recv()
-        mine = chip_sum[2 * j].astype(jnp.float32) + from_y[j].astype(jnp.float32)
-
-        @pl.when(at.outer)
-        def _():
-            to_z[target] = mine.astype(jnp.bfloat16)
-
-        @pl.when(at.inner)
-        def _():
-            z_arrival(target, direction).wait_recv()
-            ahead = from_z[(direction + 1) // 2, target].astype(jnp.float32)
-            to_z[target] = (mine + ahead).astype(jnp.bfloat16)
-
-        z_sum(target, direction).start()
+        for k, piece in enumerate(pieces):
+            y_sum(2 * j + 1, k).wait_recv()
+            mine = chip_sum[2 * j, piece].astype(jnp.float32) + from_y[j, piece].astype(
+                jnp.float32
+            )
+
+            @pl.when(at.outer)
+            def _():
+                to_z[target, piece] = mine.astype(jnp.bfloat16)
+
+            @pl.when(at.inner)
+            def _():
+                z_arrival(target, direction, k).wait_recv()
+                ahead = from_z[(direction + 1) // 2, target, piece].astype(jnp.float32)
+                to_z[target, piece] = (mine + ahead).astype(jnp.bfloat16)
+
+            z_sum(target, direction, k).start()
+        later[1 + place]()
 
     def finish():
-        y_sum(1).wait_recv()
-        part_own[...] = chip_sum[0].astype(jnp.float32) + from_y[0].astype(jnp.float32)
-        z_arrival(at.z, -at.toward).wait_recv()
-        part_own[...] += from_z[(1 - at.toward) // 2, at.z].astype(jnp.float32)
-
-        @pl.when(at.inner)
-        def _():
-            z_arrival(at.z, at.toward).wait_recv()
-            part_own[...] += from_z[(1 + at.toward) // 2, at.z].astype(jnp.float32)
+        for k, piece in enumerate(pieces):
+            y_sum(1, k).wait_recv()
+            part_own[piece] = chip_sum[0, piece].astype(jnp.float32) + from_y[0, piece].astype(
+                jnp.float32
+            )
+            z_arrival(at.z, -at.toward, k).wait_recv()
+            part_own[piece] += from_z[(1 - at.toward) // 2, at.z, piece].astype(jnp.float32)
+
+            @pl.when(at.inner)
+            def _():
+                z_arrival(at.z, at.toward, k).wait_recv()
+                part_own[piece] += from_z[(1 + at.toward) // 2, at.z, piece].astype(jnp.float32)
 
         return part_own[...]
 
@@ -527,13 +544,15 @@
             @pl.when(lax.rem(i, 2) == 1)
             def _():
                 pass_y(at.source(i // 2)).wait_send()
-                y_sum(i).wait_send()
+                for k in range(4):
+                    y_sum(i, k).wait_send()
 
             return carried
 
         lax.fori_loop(0, 8, drain_chip, 0)
         for j in (1, 2, 3):
-            z_sum(at.source(j), direction_of(j)).wait_send()
+            for k in range(4):
+                z_sum(at.source(j), direction_of(j), k).wait_send()
 
     return finish, drain
 
@@ -807,6 +826,7 @@
         self.rows = pl.ds(low, high - low)
         self.top = pl.ds(low, middle - low)
         self.bottom = pl.ds(middle, high - middle)
+        self.by_x, self.by_y = middle > low, high > middle
 
     def mine(self, z, y, x, rows):
         return self.held.at[self.at.core, z * 2 + y, x, rows]
@@ -901,19 +921,21 @@
             for y in (0, 1):
                 for x in (0, 1):
                     self.add(z, y, x, self.rows, self.sib_in[z * 2 + y, x, self.rows])
-            self.x_half(z).start()
-            self.y_half(z).start()
+            (self.x_half if self.by_x else self.y_full)(z).start()
+            (self.y_half if self.by_y else self.x_full)(z).start()
 
     def pair_up(self):
         at = self.at
         for j in (3, 2, 1, 0):
             z = at.source(j)
-            self.x_half(z).wait_recv()
-            self.add(z, 1 - at.y, self.x, self.top, self.xh_in[z, self.top])
-            self.y_full(z).start()
-            self.y_half(z).wait_recv()
-            self.add(z, at.y, 1 - self.x, self.bottom, self.yh_in[z, self.bottom])
-            self.x_full(z).start()
+            if self.by_x:
+                self.x_half(z).wait_recv()
+                self.add(z, 1 - at.y, self.x, self.top, self.xh_in[z, self.top])
+                self.y_full(z).start()
+            if self.by_y:
+                self.y_half(z).wait_recv()
+                self.add(z, at.y, 1 - self.x, self.bottom, self.yh_in[z, self.bottom])
+                self.x_full(z).start()
 
     def collect(self):
         at = self.at
@@ -940,8 +962,12 @@
     def drain(self):
         for j in range(4):
             z = self.at.source(j)
-            for copy in (self.sib, self.x_half, self.y_half, self.x_full, self.y_full):
+            for copy in (self.sib, self.x_full, self.y_full):
                 copy(z).wait_send()
+            if self.by_x:
+                self.x_half(z).wait_send()
+            if self.by_y:
+                self.y_half(z).wait_send()
             if j > 0:
                 self.z_part(z).wait_send()
 
@@ -1163,6 +1189,7 @@
             r.up_keep[half, chip] = up.astype(jnp.bfloat16)
             bend = jnp.tanh(gelu_c * (gate + 0.044715 * gate * gate * gate))
             hidden = (0.5 * gate * (1.0 + bend) * up).astype(jnp.bfloat16)
+            r.hidden_keep[half, chip] = hidden
             part = nn(hidden, downs[half][...])
             total = part if total is None else total + part
         return total[:128], total[128:]
@@ -1179,14 +1206,9 @@
     r.gain_sum[:, gain_edges[5] : gain_edges[6]] = gain_grad
     r.held[1, at.f, core] = ffn_grad.astype(jnp.bfloat16)
     own_grads = (r.gate_grad, r.up_grad, r.down_grad)
-    grads = (own_grads, tuple(r.peer_sum.at[k] for k in range(3)))
-    for half in (0, 1):
-        for target in grads[half]:
-            target[...] = jnp.zeros(target.shape, jnp.float32)
 
     def backward(chip):
         rows = rows_of(1, chip)
-        ahead = rows_of(0, chip)
         total = None
         for half in (0, 1):
             dhidden = nt(rows, downs[half][...])
@@ -1198,27 +1220,49 @@
             slope = 0.5 * (1.0 + bend) + 0.5 * gate * (1.0 - bend * bend) * (
                 gelu_c * (1.0 + 3 * 0.044715 * square)
             )
-            hidden = (unit * up).astype(jnp.bfloat16)
             dgate = (dhidden * up * slope).astype(jnp.bfloat16)
             dup = (dhidden * unit).astype(jnp.bfloat16)
             part = nn(dgate, gates[half][...]) + nn(dup, ups[half][...])
             total = part if total is None else total + part
-            gate_sum, up_sum, down_sum = grads[half]
-            gate_sum[...] += tn(dgate, ahead)
-            up_sum[...] += tn(dup, ahead)
-            down_sum[...] += tn(hidden, rows)
+            r.gate_keep[half, chip] = dgate
+            r.up_keep[half, chip] = dup
         return total[:128], total[128:]
 
     def x_copy(k):
         return remote(r.peer_w.at[k], r.from_x.at[k], x_out.at[k], x_in.at[k], at.over_x)
 
-    def send_x():
+    kept = ((r.gate_keep, 0), (r.up_keep, 0), (r.hidden_keep, 1))
+
+    def weight_grad(k, half):
+        left, which = kept[k]
+        total = None
+        for chip in range(8):
+            part = tn(left[half, chip], rows_of(which, chip))
+            total = part if total is None else total + part
+        return total
+
+    def peers():
         for k in range(3):
-            r.peer_w[k] = r.peer_sum[k].astype(jnp.bfloat16)
+            r.peer_w[k] = weight_grad(k, 1).astype(jnp.bfloat16)
             x_copy(k).start()
 
+    def own(k):
+        def step():
+            own_grads[k][...] = weight_grad(k, 0)
+
+        return step
+
     finish, drain = exchange_pass(
-        at, grad_all, bwd_gather, bwd_sum, sum_bufs, r.part_own, backward, 0, None, send_x
+        at,
+        grad_all,
+        bwd_gather,
+        bwd_sum,
+        sum_bufs,
+        r.part_own,
+        backward,
+        0,
+        None,
+        (peers, own(0), own(1), own(2)),
     )
     normed_grad = finish()
     drain()
@@ -1388,7 +1432,7 @@
         "held": ((2, 8, 2, rows, width), b16),
         "gate_keep": ((2, 8, 2 * rows, units), b16),
         "up_keep": ((2, 8, 2 * rows, units), b16),
-        "peer_sum": ((3, units, width), f32),
+        "hidden_keep": ((2, 8, 2 * rows, units), b16),
         "part_own": ((rows, width), f32),
         "to_sib": ((8, rows, width), b16),
         "from_sib": ((8, rows, width), b16),
@@ -1411,7 +1455,7 @@
         "gain_in": ((7, 1, 5120), f32),
     }
     gather_sems = [DMA((2,)), DMA((4,)), DMA((4,)), DMA((4,)), DMA((4,)), DMA((8,)), DMA((8,))]
-    sum_sems = [DMA((8,)), DMA((8,)), DMA((4,)), DMA((4,)), DMA((4,)), DMA((2, 4))]
+    sum_sems = [DMA((8,)), DMA((8,)), DMA((4, 4)), DMA((4, 4)), DMA((4, 4)), DMA((2, 4, 4))]
     front_sems = gain_sems() + gather_weight_sems() + [DMA((3,))] * 4
     ffn_sems = (gather_sems + sum_sems) * 2 + [DMA((3,)), DMA((3,))]
     back_sems = [DMA((2, 4))] * 12 + [DMA((2,)), DMA((2,)), DMA((6,)), DMA((7,))]

time: 241 us -> 227 us (0.942)
  Pallas kernels: 236 us -> 223 us
    pallas_call x1, Pallas kernels: 232 us -> 219 us  [layer_call(): pl.pallas_call(kernel, out_shape=tuple((jax.ShapeDtypeStruct(*spec) for s...]
where the time goes in v5:
time: 227 us
  Pallas kernels  223 us (98%)
    pallas_call x1, Pallas kernels, layer_call(): pl.pallas_call(kernel, out_shape=tuple((jax.ShapeDtypeStruct(*spec) for s...  219 us

profile of v5, /device:TPU:0, one launch (start us, length us, event | category | flops | bytes accessed | tf_op | source)
XLA Modules:
  0.0 226.5 jit_solution(14755504400345764380)
XLA Ops:
  0.7 0.0 copy-start.1
  0.7 0.6 copy-done.1
  1.3 0.0 copy-start.2
  1.3 0.6 copy-done.2
  2.0 0.1 dynamic_update_slice.3.refs_2_
  2.1 0.0 copy-start
  2.1 0.7 copy.21.refs_1_
  2.8 0.0 copy-done
  2.8 1.0 multiply_sine_fusion
  3.8 218.6 %layer.1 = (bf16[128,1152]{1,0:T(8,128)(2,1)}, f32[128,1152]{1,0:T(8,128)}, f32[1,256]{1,0:T(1,128)}, f32[32,1152]{1,0:T(8,128)}, f32[8,1152]{1,0:T(8,128)}, /*i...) custom-call(bf16[128,1152]{1,0:T(8,128)(2,1)} %refs_0_.1, ...), custom_call_target="tpu_custom_call" | custom-call | tf_op jit(solution)/shard_map/layer/pallas_call | solution.py:1476
  222.4 4.0 %settle.1 = (bf16[128,1152]{1,0:T(8,128)(2,1)}, f32[128,1152]{1,0:T(8,128)}, f32[1,256]{1,0:T(1,128)}, f32[32,1152]{1,0:T(8,128)}, f32[8,1152]{1,0:T(8,128)}, /*...) custom-call(bf16[128,1152]{1,0:T(8,128)(2,1)} %get-tuple-element.30., ...), custom_call_target="tpu_custom_call" | custom-call | tf_op jit(solution)/shard_map/settle/pallas_call | solution.py:1505
  (4 shorter events, 0.0 us)
Async XLA Ops:
  0.7 0.7 copy-start.1
  1.3 0.7 copy-start.2
  2.1 0.8 copy-start

commit v6 on v5

--- a/solution.py
+++ b/solution.py
@@ -330,7 +330,7 @@
     entry = pltpu.get_barrier_semaphore()
     for partner in partners:
         pl.semaphore_signal(entry, inc=1, device_id=partner, device_id_type=MESH)
-    pl.semaphore_wait(entry, len(partners))
+    return entry
 
 
 def exchange_pass(at, held, gather_sems, sum_sems, sum_bufs, part_own, compute, lag=0, ready=None, then=()):
@@ -392,8 +392,8 @@
     def sib_sum(i):
         return remote(to_sib.at[i], from_sib.at[i], t_out.at[i], t_in.at[i], at.sibling)
 
-    rows = part_own.shape[0] // 4
-    pieces = [pl.ds(k * rows, rows) for k in range(4)]
+    rows = part_own.shape[0] // 2
+    pieces = [pl.ds(k * rows, rows) for k in range(2)]
 
     def y_sum(i, k):
         return remote(
@@ -405,7 +405,7 @@
         )
 
     def send_y(i):
-        for k in range(4):
+        for k in range(2):
             y_sum(i, k).start()
 
     def finish_chip(i):
@@ -544,14 +544,14 @@
             @pl.when(lax.rem(i, 2) == 1)
             def _():
                 pass_y(at.source(i // 2)).wait_send()
-                for k in range(4):
+                for k in range(2):
                     y_sum(i, k).wait_send()
 
             return carried
 
         lax.fori_loop(0, 8, drain_chip, 0)
         for j in (1, 2, 3):
-            for k in range(4):
+            for k in range(2):
                 z_sum(at.source(j), direction_of(j), k).wait_send()
 
     return finish, drain
@@ -559,6 +559,7 @@
 
 gain_edges = (0, 1152, 1408, 1664, 2816, 3968, 5120)
 score_step = 0.0625
+log_base = 13.815510557964274
 hidden_score = -1e30
 
 
@@ -697,10 +698,10 @@
 
     def begin(self):
         self.x_copy(self.x).start()
+        self.y_first(self.at.y, self.x).start()
 
     def spread(self):
         at = self.at
-        self.y_first(at.y, self.x).start()
         self.x_copy(1 - self.x).wait_recv()
         self.own(at.toward, 0).start()
 
@@ -1040,16 +1041,22 @@
     early = WeightGather(at, w_all, w_sems, 0, 0, 48)
     late = WeightGather(at, w_all, w_sems, 1, 48, 80)
     chip = at.f * 2 + s // 2
+    entry = greet(
+        [at.sibling, at.over_x, at.over_y]
+        + [at.at_z(lax.rem(at.z + step, 4)) for step in (1, 2, 3)]
+    )
     w_all[chip, core, 0:32] = r.own_q[...]
     w_all[chip, core, 32:48] = jnp.concatenate(
         [r.own_k[...].astype(jnp.float32), r.own_v[...].astype(jnp.float32)], axis=0
     ).astype(jnp.bfloat16)
     w_all[chip, core, 48:80] = r.own_o[...]
-    r.gain_all[at.f * 4 + s] = r.gain_row[...]
-    greet(
-        [at.sibling, at.over_x, at.over_y]
-        + [at.at_z(lax.rem(at.z + step, 4)) for step in (1, 2, 3)]
-    )
+    device = at.f * 4 + s
+    share = jnp.concatenate(
+        [r.own_gains[...].astype(jnp.float32).reshape(1, 160), jnp.zeros((1, 96), jnp.float32)],
+        axis=1,
+    )
+    r.gain_all[device] = pltpu.roll(share, lax.rem(device, 4) * 32, 1)
+    pl.semaphore_wait(entry, 6)
     def x_weight(k):
         ref = (r.own_gate, r.own_up, r.own_down)[k]
         return remote(ref, r.peer_w.at[k], x_out.at[k], x_in.at[k], at.over_x)
@@ -1070,22 +1077,33 @@
     x_weight(0).start()
     x_weight(1).start()
     gain_step(1)()
-    early.walk((gain_step(2), gain_step(3), late.spread))
-    placed = r.gain_all[...].reshape(32, 256)
-    pieces = []
-    for m in range(8):
-        for k in range(5):
-            piece = None
-            if k < 4:
-                piece = placed[4 * m + k : 4 * m + k + 1, :128]
-            if k > 0:
-                other = placed[4 * m + k - 1 : 4 * m + k, 128:]
-                piece = other if piece is None else piece + other
-            pieces.append(piece)
-    r.gains[...] = jnp.concatenate(pieces, axis=1)
+    starts = jnp.broadcast_to(r.doc[...].astype(jnp.float32).reshape(1, 128), (128, 128)).T
+    r.starts[...] = starts
+    place = (lax.broadcasted_iota(jnp.int32, (128, 128), 0) + s * 128).astype(jnp.float32)
+    step = lax.broadcasted_iota(jnp.int32, (128, 128), 1).astype(jnp.float32)
+    angle = (place - starts) * jnp.exp(step * (-2.0 / 256 * log_base))
+    r.cos[...] = jnp.cos(angle)
+    r.sin[...] = jnp.sin(angle)
+
+    def first_norm():
+        late.spread()
+        placed = r.gain_all[...].reshape(32, 256)
+        pieces = []
+        for m in range(8):
+            for k in range(5):
+                piece = None
+                if k < 4:
+                    piece = placed[4 * m + k : 4 * m + k + 1, :128]
+                if k > 0:
+                    other = placed[4 * m + k - 1 : 4 * m + k, 128:]
+                    piece = other if piece is None else piece + other
+                pieces.append(piece)
+        r.gains[...] = jnp.concatenate(pieces, axis=1)
+        gain = gain_parts(r)
+        residual = r.tokens[...].astype(jnp.float32)
+        r.normed[...] = (residual * rms_scale(residual) * gain[0]).astype(jnp.bfloat16)
+    early.walk((gain_step(2), gain_step(3), first_norm))
     gain = gain_parts(r)
-    residual = r.tokens[...].astype(jnp.float32)
-    r.normed[...] = (residual * rms_scale(residual) * gain[0]).astype(jnp.bfloat16)
     early.settle()
     normed = r.normed[...]
     cos, sin = r.cos[...], r.sin[...]
@@ -1125,7 +1143,8 @@
     keys, values = kv_parts(r)
     key_place = lax.broadcasted_iota(jnp.int32, (128, 512), 1)
     query_place = lax.broadcasted_iota(jnp.int32, (128, 512), 0) + s * 128
-    allowed = (key_place >= r.doc[...]) & (key_place <= query_place)
+    starts = jnp.concatenate([r.starts[...]] * 4, axis=1).astype(jnp.int32)
+    allowed = (key_place >= starts) & (key_place <= query_place)
     for head in range(4):
         raw = nt(r.query[:, columns_of(head)], keys) * score_step
         scores = jnp.where(allowed, raw, hidden_score)
@@ -1197,14 +1216,20 @@
     finish, drain = exchange_pass(
         at, normed_all, fwd_gather, fwd_sum, sum_bufs, r.part_own, forward, 0, weights_here
     )
-    ffn_raw = finish()
-    drain()
     gain = gain_parts(r)[5]
-    scale = rms_scale(ffn_raw)
-    r.result[...] = (r.middle[...] + ffn_raw * scale * gain).astype(jnp.bfloat16)
-    ffn_grad, gain_grad = norm_back(ffn_raw, gain, r.cotangent[...].astype(jnp.float32))
-    r.gain_sum[:, gain_edges[5] : gain_edges[6]] = gain_grad
+    upstream = r.cotangent[...].astype(jnp.float32)
+    ffn_grad, _ = norm_back(finish(), gain, upstream)
     r.held[1, at.f, core] = ffn_grad.astype(jnp.bfloat16)
+    drain_forward = drain
+
+    def write_result():
+        ffn_raw = r.part_own[...]
+        normed = ffn_raw * rms_scale(ffn_raw)
+        r.result[...] = (r.middle[...] + normed * gain).astype(jnp.bfloat16)
+        share = jnp.sum(r.cotangent[...].astype(jnp.float32) * normed, axis=0, keepdims=True)
+        r.gain_sum[:, gain_edges[5] : gain_edges[6]] = share
+        drain_forward()
+
     own_grads = (r.gate_grad, r.up_grad, r.down_grad)
 
     def backward(chip):
@@ -1261,7 +1286,7 @@
         r.part_own,
         backward,
         0,
-        None,
+        write_result,
         (peers, own(0), own(1), own(2)),
     )
     normed_grad = finish()
@@ -1286,6 +1311,18 @@
     outer = WeightReturn(at, r.held, bufs, w_sems, 1, 48, 64, 80)
     inner = WeightReturn(at, r.held, bufs, w_sems, 0, 0, 16, 48)
     gain_total = GainSum(at, r.gain_sum, r.gain_out, r.gain_in, sems[14:16])
+
+    def write(k):
+        source, target = (
+            (r.result, r.result_out),
+            (r.token_grad, r.token_grad_out),
+            (r.gate_grad, r.gate_grad_out),
+            (r.up_grad, r.up_grad_out),
+            (r.down_grad, r.down_grad_out),
+        )[k]
+        return pltpu.make_async_copy(source, target, sems[16].at[k])
+
+    write(0).start()
 
     def put_gain(k, value):
         r.gain_sum[:, gain_edges[k] : gain_edges[k + 1]] = value
@@ -1366,10 +1403,14 @@
     put_gain(0, gain_grad)
     gain_total.send(0)
     r.token_grad[...] = r.middle[...] + part
+    write(1).start()
     inner.merge()
     gain_total.take(0)
     gain_total.send(1)
     outer.collect()
+    complete()
+    for k in (2, 3, 4):
+        write(k).start()
     inner.pair_up()
     gain_total.take(1)
     gain_total.send(2)
@@ -1377,7 +1418,6 @@
     gain_total.take(2)
     gain_total.send(3)
     r.o_grad[...] = outer.total()
-    complete()
     total = inner.total()
     r.q_grad[...] = total[:32]
     r.k_grad[...] = total[32:40]
@@ -1390,6 +1430,8 @@
     )
     outer.drain()
     inner.drain()
+    for k in range(5):
+        write(k).wait()
     gain_total.drain()
     kv_sib.wait_send()
     kv_x.wait_send()
@@ -1415,6 +1457,9 @@
         "gain_sum": ((1, 5120), f32),
         "w_all": ((16, 2, 80, width), b16),
         "gain_all": ((32, 1, 256), f32),
+        "starts": ((rows, rows), f32),
+        "cos": ((rows, rows), f32),
+        "sin": ((rows, rows), f32),
         "gains": ((1, 5120), f32),
         "wk": ((256, width), b16),
         "wv": ((256, width), b16),
@@ -1455,12 +1500,15 @@
         "gain_in": ((7, 1, 5120), f32),
     }
     gather_sems = [DMA((2,)), DMA((4,)), DMA((4,)), DMA((4,)), DMA((4,)), DMA((8,)), DMA((8,))]
-    sum_sems = [DMA((8,)), DMA((8,)), DMA((4, 4)), DMA((4, 4)), DMA((4, 4)), DMA((2, 4, 4))]
+    sum_sems = [DMA((8,)), DMA((8,)), DMA((4, 2)), DMA((4, 2)), DMA((4, 2)), DMA((2, 4, 2))]
     front_sems = gain_sems() + gather_weight_sems() + [DMA((3,))] * 4
     ffn_sems = (gather_sems + sum_sems) * 2 + [DMA((3,)), DMA((3,))]
-    back_sems = [DMA((2, 4))] * 12 + [DMA((2,)), DMA((2,)), DMA((6,)), DMA((7,))]
+    back_sems = [DMA((2, 4))] * 12 + [DMA((2,)), DMA((2,)), DMA((6,)), DMA((7,)), DMA((5,))]
     sems = front_sems + ffn_sems + back_sems
-    names = tuple(values) + tuple(outs) + tuple(scratch)
+    large = ("result", "token_grad", "gate_grad", "up_grad", "down_grad")
+    scratch.update({name: outs[name] for name in large})
+    names = tuple(values) + tuple(name + "_out" if name in large else name for name in outs)
+    names += tuple(scratch)
 
     def kernel(*refs):
         at = Place()
@@ -1477,7 +1525,9 @@
         kernel,
         out_shape=tuple(jax.ShapeDtypeStruct(*spec) for spec in outs.values()),
         in_specs=[vmem] * len(values),
-        out_specs=tuple([vmem] * len(outs)),
+        out_specs=tuple(
+            pl.BlockSpec(memory_space=pl.ANY) if name in large else vmem for name in outs
+        ),
         scratch_shapes=[pltpu.VMEM(*spec) for spec in scratch.values()] + sems,
         compiler_params=pltpu.CompilerParams(
             collective_id=1, has_side_effects=True, vmem_limit_bytes=63 << 20
@@ -1515,21 +1565,12 @@
 def one_kernel(
     tokens, doc_start, gains, w_query, w_key, w_value, w_out, w_gate, w_up, w_down, cotangent
 ):
-    rows = tokens.shape[0]
-    device = lax.axis_index("fsdp") * lax.axis_size("seq") + lax.axis_index("seq")
     share = gains.shape[0]
-    gain_row = lax.dynamic_update_slice(
-        jnp.zeros((1, 256), jnp.float32),
-        gains[None].astype(jnp.float32),
-        (0, lax.rem(device, 4) * 32),
-    )
-    places = lax.axis_index("seq") * rows + jnp.arange(rows, dtype=jnp.int32) - doc_start
-    cos, sin = rope_tables(places, 256)
     out = layer_call(
         {
             "tokens": tokens,
-            "doc": doc_start[:, None],
-            "gain_row": gain_row,
+            "doc": doc_start,
+            "own_gains": gains,
             "own_q": w_query.T,
             "own_k": w_key.T,
             "own_v": w_value.T,
@@ -1537,8 +1578,6 @@
             "own_gate": w_gate.T,
             "own_up": w_up.T,
             "own_down": w_down,
-            "cos": cos[:, 0],
-            "sin": sin[:, 0],
             "cotangent": cotangent,
         }
     )

time: 227 us -> 224 us (0.987)
  no operation moved by 1% of the time
where the time goes in v6:
time: 224 us
  Pallas kernels  223 us (100%)
    pallas_call x1, Pallas kernels, layer_call(): pl.pallas_call(kernel, out_shape=tuple((jax.ShapeDtypeStruct(*spec) for s...  219 us

profile of v6, /device:TPU:0, one launch (start us, length us, event | category | flops | bytes accessed | tf_op | source)
XLA Modules:
  0.0 224.0 jit_solution(1539460425880497917)
XLA Ops:
  0.6 219.2 %layer.1 = (bf16[128,1152]{1,0:T(8,128)(2,1)}, f32[128,1152]{1,0:T(8,128)}, f32[1,256]{1,0:T(1,128)}, f32[32,1152]{1,0:T(8,128)}, f32[8,1152]{1,0:T(8,128)}, /*i...) custom-call(bf16[128,1152]{1,0:T(8,128)(2,1)} %refs_0_.1, ...), custom_call_target="tpu_custom_call" | custom-call | tf_op jit(solution)/shard_map/layer/pallas_call | solution.py:1524
  219.8 4.0 %settle.1 = (bf16[128,1152]{1,0:T(8,128)(2,1)}, f32[128,1152]{1,0:T(8,128)}, f32[1,256]{1,0:T(1,128)}, f32[32,1152]{1,0:T(8,128)}, f32[8,1152]{1,0:T(8,128)}, /*...) custom-call(bf16[128,1152]{1,0:T(8,128)(2,1)} %get-tuple-element.30., ...), custom_call_target="tpu_custom_call" | custom-call | tf_op jit(solution)/shard_map/settle/pallas_call | solution.py:1555

commit v7 on v6

--- a/solution.py
+++ b/solution.py
@@ -392,8 +392,8 @@
     def sib_sum(i):
         return remote(to_sib.at[i], from_sib.at[i], t_out.at[i], t_in.at[i], at.sibling)
 
-    rows = part_own.shape[0] // 2
-    pieces = [pl.ds(k * rows, rows) for k in range(2)]
+    rows = part_own.shape[0] // 4
+    pieces = [pl.ds(k * rows, rows) for k in range(4)]
 
     def y_sum(i, k):
         return remote(
@@ -405,7 +405,7 @@
         )
 
     def send_y(i):
-        for k in range(2):
+        for k in range(4):
             y_sum(i, k).start()
 
     def finish_chip(i):
@@ -544,14 +544,14 @@
             @pl.when(lax.rem(i, 2) == 1)
             def _():
                 pass_y(at.source(i // 2)).wait_send()
-                for k in range(2):
+                for k in range(4):
                     y_sum(i, k).wait_send()
 
             return carried
 
         lax.fori_loop(0, 8, drain_chip, 0)
         for j in (1, 2, 3):
-            for k in range(2):
+            for k in range(4):
                 z_sum(at.source(j), direction_of(j), k).wait_send()
 
     return finish, drain
@@ -910,10 +910,6 @@
         self.held[core, f, x, rows] = (
             self.held[core, f, x, rows].astype(jnp.float32) + more.astype(jnp.float32)
         ).astype(jnp.bfloat16)
-
-    def send_sib(self):
-        for j in (3, 2, 1, 0):
-            self.sib(self.at.source(j)).start()
 
     def merge(self):
         for j in (3, 2, 1, 0):
@@ -1342,7 +1338,7 @@
     attn_grad = attn_grad.astype(jnp.bfloat16)
     for head in range(4):
         put_rows(head, 48, 32, tn(r.mixed[:, columns_of(head)], attn_grad))
-    outer.send_sib()
+        outer.sib(head).start()
     keys, values = kv_parts(r)
     for head in range(4):
         mixed_grad = nt(attn_grad, rows_of_head(r.w_all, head, 48, 32)).astype(jnp.bfloat16)
@@ -1395,7 +1391,7 @@
     woven = (nn(k_raw_grad, pick(0)) + nn(v_raw_grad, pick(8))).astype(jnp.bfloat16)
     for head in range(4):
         put_rows(head, 32, 16, tn(woven[:, 128 * head : 128 * head + 128], normed))
-    inner.send_sib()
+        inner.sib(head).start()
     normed_grad = nn(k_raw_grad, r.wk[...]) + nn(v_raw_grad, r.wv[...])
     for head in range(4):
         normed_grad += nn(r.query[:, columns_of(head)], rows_of_head(r.w_all, head, 0, 32))
@@ -1500,7 +1496,7 @@
         "gain_in": ((7, 1, 5120), f32),
     }
     gather_sems = [DMA((2,)), DMA((4,)), DMA((4,)), DMA((4,)), DMA((4,)), DMA((8,)), DMA((8,))]
-    sum_sems = [DMA((8,)), DMA((8,)), DMA((4, 2)), DMA((4, 2)), DMA((4, 2)), DMA((2, 4, 2))]
+    sum_sems = [DMA((8,)), DMA((8,)), DMA((4, 4)), DMA((4, 4)), DMA((4, 4)), DMA((2, 4, 4))]
     front_sems = gain_sems() + gather_weight_sems() + [DMA((3,))] * 4
     ffn_sems = (gather_sems + sum_sems) * 2 + [DMA((3,)), DMA((3,))]
     back_sems = [DMA((2, 4))] * 12 + [DMA((2,)), DMA((2,)), DMA((6,)), DMA((7,)), DMA((5,))]

time: 224 us -> 221 us (0.987)
  Pallas kernels: 223 us -> 220 us
    pallas_call x1, Pallas kernels: 219 us -> 216 us  [layer_call(): pl.pallas_call(kernel, out_shape=tuple((jax.ShapeDtypeStruct(*spec) for s...]
where the time goes in v7:
time: 221 us
  Pallas kernels  220 us (100%)
    pallas_call x1, Pallas kernels, layer_call(): pl.pallas_call(kernel, out_shape=tuple((jax.ShapeDtypeStruct(*spec) for s...  216 us

profile of v7, /device:TPU:0, one launch (start us, length us, event | category | flops | bytes accessed | tf_op | source)
XLA Modules:
  0.0 220.9 jit_solution(2235303926680378965)
XLA Ops:
  0.6 216.0 %layer.1 = (bf16[128,1152]{1,0:T(8,128)(2,1)}, f32[128,1152]{1,0:T(8,128)}, f32[1,256]{1,0:T(1,128)}, f32[32,1152]{1,0:T(8,128)}, f32[8,1152]{1,0:T(8,128)}, /*i...) custom-call(bf16[128,1152]{1,0:T(8,128)(2,1)} %refs_0_.1, ...), custom_call_target="tpu_custom_call" | custom-call | tf_op jit(solution)/shard_map/layer/pallas_call | solution.py:1520
  216.7 4.0 %settle.1 = (bf16[128,1152]{1,0:T(8,128)(2,1)}, f32[128,1152]{1,0:T(8,128)}, f32[1,256]{1,0:T(1,128)}, f32[32,1152]{1,0:T(8,128)}, f32[8,1152]{1,0:T(8,128)}, /*...) custom-call(bf16[128,1152]{1,0:T(8,128)(2,1)} %get-tuple-element.30., ...), custom_call_target="tpu_custom_call" | custom-call | tf_op jit(solution)/shard_map/settle/pallas_call | solution.py:1551
